TPU v7x, 256 devices: a whole 4x4x8 slice. The times are simulated.
256 devices in a mesh: dp: 8 (over y, core), tower: 32 (over x, z).
Axes of the slice: x: 4, y: 4, z: 8, core: 2. Of those that a mesh axis runs over, the one named last changes fastest.
Arguments:
- attn_out: bfloat16 [32768, 4096], P(('dp', 'tower')), may hold values from -0.375 to 0.375
- out_cot: bfloat16 [32768, 4096], P(('dp', 'tower')), may hold values from -6 to 6
- modality: int32 [32768], P(('dp', 'tower')), may hold values from 0 to 2, as said below
- group_modality: int32 [8], replicated, may hold values from 0 to 2, as said below
- o_weight: bfloat16 [32768, 4096], P('tower'), as said below
Outputs:
- attn_grad: bfloat16 [32768, 4096], P(('dp', 'tower'))
- weight_grad: bfloat16 [32768, 4096], P('tower', 'dp')
Inputs may be any that keep to these rules, and one draw needn't show every extreme that they name: `group_modality`: every modality is served by at least one group. In each block of 128 tokens (one device's tokens), a modality served by k groups appears at most k * 24 times; in every block the modality served by the fewest groups (the lowest such id on a tie) appears exactly that often. `o_weight`: groups that serve the same modality hold equal rows.
All inputs are finite; a program needn't handle non-finite values.
Results may differ from a plain program's by a relative error of at most 0.014.
Values may be sent and summed in bfloat16 or wider, within the bound.
A program may use at most 128 MiB of HBM per device.

v0:
```python
import jax
import jax.numpy as jnp
from jax import lax
from jax.sharding import PartitionSpec as P

NGROUP = 8
CAP = 24


def routing(modal_rows, tower_idx, group_modality):
    modal_ids = jnp.arange(3, dtype=jnp.int32)
    member = (modal_rows[:, None] == modal_ids[None, :]).astype(jnp.int32)
    before = jnp.cumsum(member, axis=0) - member
    order_in = jnp.sum(before * member, axis=1)
    group_of = (group_modality[:, None] == modal_ids[None, :]).astype(jnp.int32)
    per_kind = jnp.sum(group_of, axis=0)
    group_rank = jnp.sum((jnp.cumsum(group_of, axis=0) - group_of) * group_of, axis=1)
    how_many = jnp.sum(member * per_kind[None, :], axis=1)
    target = (order_in + tower_idx) % how_many
    chosen = (group_modality[None, :] == modal_rows[:, None]) & (
        group_rank[None, :] == target[:, None]
    )
    group_ids = jnp.arange(group_modality.shape[0], dtype=jnp.int32)
    routed = jnp.sum(chosen.astype(jnp.int32) * group_ids[None, :], axis=1)
    slot_idx = order_in // how_many
    return (routed, slot_idx)


def per_device(attn_out, out_cot, modality, group_modality, o_weight):
    tower_idx = lax.axis_index("tower")
    tower_count = lax.axis_size("tower")
    group_size = tower_count // NGROUP
    piece_rows = o_weight.shape[0]
    model_width = attn_out.shape[1]
    tok_count = attn_out.shape[0]
    first_col = tower_idx % group_size * piece_rows
    routed, slot_idx = routing(modality, tower_idx, group_modality)
    group_ids = jnp.arange(NGROUP, dtype=jnp.int32)
    slot_ids = jnp.arange(CAP, dtype=jnp.int32)
    dispatch = (
        (routed[None, None, :] == group_ids[:, None, None])
        & (slot_idx[None, None, :] == slot_ids[None, :, None])
    ).astype(jnp.bfloat16)
    cot_group = jnp.einsum(
        "gct,te->gce", dispatch, out_cot, preferred_element_type=jnp.float32
    ).astype(jnp.bfloat16)
    cot_send = jnp.broadcast_to(cot_group[:, None], (NGROUP, group_size, CAP, model_width)).reshape(
        tower_count, CAP, model_width
    )
    attn_group = jnp.einsum(
        "gct,te->gce", dispatch, attn_out, preferred_element_type=jnp.float32
    ).astype(jnp.bfloat16)
    attn_send = jnp.broadcast_to(
        attn_group[:, None], (NGROUP, group_size, CAP, model_width)
    ).reshape(tower_count, CAP, model_width)
    attn_got = lax.all_to_all(attn_send, "tower", split_axis=0, concat_axis=0, tiled=True)
    cot_got = lax.all_to_all(cot_send, "tower", split_axis=0, concat_axis=0, tiled=True)
    attn_use = lax.dynamic_slice_in_dim(attn_got, first_col, piece_rows, 2)
    grad_piece = lax.dot_general(
        cot_got, o_weight, (((2,), (1,)), ((), ())), preferred_element_type=jnp.float32
    ).astype(jnp.bfloat16)
    returned = lax.all_to_all(grad_piece, "tower", split_axis=0, concat_axis=0, tiled=True)
    returned, attn_use, cot_got = (returned, attn_use, cot_got)
    returned_groups = returned.reshape(NGROUP, group_size, CAP, piece_rows)
    attn_grad = jnp.einsum(
        "gct,gpce->tpe", dispatch, returned_groups, preferred_element_type=jnp.float32
    )
    attn_grad = attn_grad.reshape(tok_count, model_width).astype(jnp.bfloat16)
    attn_rows = attn_use.reshape(tower_count * CAP, piece_rows)
    cot_rows = cot_got.reshape(tower_count * CAP, model_width)
    summed = lax.psum_scatter(
        lax.dot_general(
            cot_rows, attn_rows, (((0,), (0,)), ((), ())), preferred_element_type=jnp.float32
        ).astype(jnp.bfloat16),
        "dp",
        scatter_dimension=0,
        tiled=True,
    ).astype(jnp.float32)
    weight_grad = summed.T.astype(jnp.bfloat16)
    return (attn_grad, weight_grad)


def solution(mesh):
    return jax.shard_map(
        per_device,
        mesh=mesh,
        in_specs=(
            P(("dp", "tower"), None),
            P(("dp", "tower"), None),
            P(("dp", "tower")),
            P(),
            P("tower", None),
        ),
        out_specs=(P(("dp", "tower"), None), P("tower", "dp")),
        check_vma=False,
    )
```

profile of v0, /device:TPU:8, one launch (start us, length us, event | category | flops | bytes accessed | tf_op | source)
XLA Modules:
  0.0 400.8 jit_solution(969259693727936235)
XLA Ops:
  7.2 0.7 fusion.19
  7.9 0.2 reduce_window_sum.22
  8.1 0.8 select_reduce_fusion.3
  8.9 0.7 fusion.12
  9.6 0.2 reduce_window_sum.23
  9.8 0.8 select_reduce_fusion
  10.7 0.1 and_select_fusion.1
  10.8 0.8 select_reduce_fusion.2
  11.6 0.6 convolution_convert_fusion.1
  12.1 3.4 broadcast_in_dim.9
  15.6 11.4 %all-to-all-start = ((bf16[32,24,4096]{2,1,0:T(8,128)(2,1)}), bf16[32,24,4096]{2,1,0:T(8,128)(2,1)}, u32[]{:S(2)}, u32[]{:S(2)}) async-start(bf16[32,24,4096]{2,1,0:T(8,128)(2,1)} %bitcast.29), calls=%async_computation | async-start | bytes 12582912 | tf_op jit(solution)/shard_map/all_to_all | solution.py:57
  27.0 1.8 convolution_convert_fusion
  28.8 137.9 %all-to-all-done = bf16[32,24,4096]{2,1,0:T(8,128)(2,1)} async-done(((bf16[32,24,4096]{2,1,0:T(8,128)(2,1)}), bf16[32,24,4096]{2,1,0:T(8,128)(2,1)}, u32[]{:S(2)}, u32[]{:S(2)}) %all-to-all-start) | async-done | bytes 6291488 | tf_op jit(solution)/shard_map/all_to_all | solution.py:57
  166.7 3.4 broadcast_in_dim.10
  170.2 9.9 %all-to-all-start.2 = ((bf16[32,24,4096]{2,1,0:T(8,128)(2,1)}), bf16[32,24,4096]{2,1,0:T(8,128)(2,1)}, u32[]{:S(2)}, u32[]{:S(2)}) async-start(bf16[32,24,4096]{2,1,0:T(8,128)(2,1)} %bitcast.28), calls=%async_computation.2 | async-start | bytes 12582912 | tf_op jit(solution)/shard_map/all_to_all | solution.py:56
  180.0 0.0 reduce-scatter.2.cloned.1.call-start
  180.1 140.0 %all-to-all-done.2 = bf16[32,24,4096]{2,1,0:T(8,128)(2,1)} async-done(((bf16[32,24,4096]{2,1,0:T(8,128)(2,1)}), bf16[32,24,4096]{2,1,0:T(8,128)(2,1)}, u32[]{:S(2)}, u32[]{:S(2)}) %all-to-all-start.2) | async-done | bytes 6291488 | tf_op jit(solution)/shard_map/all_to_all | solution.py:56
  320.1 11.3 %bitcast_convert_fusion = bf16[4096,1024]{1,0:T(8,128)(2,1)} fusion(bf16[32,24,4096]{2,1,0:T(8,128)(2,1)} %all-to-all-done, bf16[32,24,4096]{2,1,0:T(8,128)(2,1)} %all-to-all-done.2, s32[]{:T(128)S(6)} %select_n.39), kind=kOutput, calls=%fused_computation | convolution fusion | flops 6446645248 | bytes 16252932 | tf_op jit(solution)/shard_map/dot_general | solution.py:72
  331.4 0.0 reduce-scatter.2.cloned.1.call-update
  331.4 11.0 %fusion.3 = bf16[32,24,1024]{2,1,0:T(8,128)(2,1)S(1)} fusion(bf16[32,24,4096]{2,1,0:T(8,128)(2,1)} %all-to-all-done, bf16[1024,4096]{1,0:T(8,128)(2,1)} %param.9), kind=kOutput, calls=%fused_computation.7 | convolution fusion | flops 6443237376 | bytes 16252928 | tf_op jit(solution)/shard_map/dot_general | solution.py:59
  342.4 47.7 %all_to_all.15 = bf16[32,24,1024]{2,1,0:T(8,128)(2,1)S(1)} all-to-all(bf16[32,24,1024]{2,1,0:T(8,128)(2,1)S(1)} %fusion.3), channel_id=1, replica_groups=mesh['dp'=8,'tower'=32] {'tower'}, dimensions={0} | all-to-all | bytes 3145728 | tf_op jit(solution)/shard_map/all_to_all | solution.py:62
  390.1 0.2 copy.17
  390.2 1.5 fusion.2
  391.7 2.3 copy.16
  (5 shorter events, 0.0 us)
Async XLA Ops:
  7.2 4.4 %copy-start = (bf16[128,4096]{1,0:T(8,128)(2,1)S(1)}, bf16[128,4096]{1,0:T(8,128)(2,1)}, u32[]{:S(2)}) copy-start(bf16[128,4096]{1,0:T(8,128)(2,1)} %param.6) | copy-start | bytes 3145732
  15.6 151.1 %all-to-all-start = ((bf16[32,24,4096]{2,1,0:T(8,128)(2,1)}), bf16[32,24,4096]{2,1,0:T(8,128)(2,1)}, u32[]{:S(2)}, u32[]{:S(2)}) async-start(bf16[32,24,4096]{2,1,0:T(8,128)(2,1)} %bitcast.29), calls=%async_computation | async-start | bytes 12582912 | tf_op jit(solution)/shard_map/all_to_all | solution.py:57
  170.2 149.9 %all-to-all-start.2 = ((bf16[32,24,4096]{2,1,0:T(8,128)(2,1)}), bf16[32,24,4096]{2,1,0:T(8,128)(2,1)}, u32[]{:S(2)}, u32[]{:S(2)}) async-start(bf16[32,24,4096]{2,1,0:T(8,128)(2,1)} %bitcast.28), calls=%async_computation.2 | async-start | bytes 12582912 | tf_op jit(solution)/shard_map/all_to_all | solution.py:56
  180.0 211.7 %reduce-scatter.2.cloned.1.call-start = ((), (), s32[]{:S(2)}) async-start(), calls=%async_computation.4 | async-start | bytes 9437184 | tf_op jit(solution)/shard_map/reduce_scatter | solution.py:71
Sparse Core Ops, SparseCore 0:
  331.5 53.2 reduce-scatter.1
where the time goes:
time: 402 us; the launch traced here: 401 us
  waiting for transfers between devices  278 us (69%)
  blocking collectives  47.7 us (12%)
  matrix products  26.1 us (6%)
  starting transfers between devices  21.3 us (5%)
  between operations  14.1 us (4%)
  local copies, waits for them, and re-layouts  9.32 us (2%)
  other arithmetic  4.36 us (1%)
    all_to_all x1, waiting for transfers between devices, per_device(): lax.all_to_all(attn_send, 'tower', split_axis=0, concat_axis=0, tiled=True)  140 us
    all_to_all x1, waiting for transfers between devices, per_device(): lax.all_to_all(cot_send, 'tower', split_axis=0, concat_axis=0, tiled=True)  138 us
    all_to_all x1, blocking collectives, per_device(): lax.all_to_all(grad_piece, 'tower', split_axis=0, concat_axis=0, tiled=True)  47.7 us
    all_to_all x1, starting transfers between devices, per_device(): lax.all_to_all(cot_send, 'tower', split_axis=0, concat_axis=0, tiled=True)  11.4 us
    dot_general x1, matrix products, per_device(): lax.dot_general(cot_rows, attn_rows, (((0,), (0,)), ((), ())), preferred_...  11.3 us
    dot_general x1, matrix products, per_device(): lax.dot_general(cot_got, o_weight, (((2,), (1,)), ((), ())), preferred_el...  11 us
    all_to_all x1, starting transfers between devices, per_device(): lax.all_to_all(attn_send, 'tower', split_axis=0, concat_axis=0, tiled=True)  9.87 us
  transfers between devices with their start and end apart: 3, of which 2 were waited for; matrix products, arithmetic and copies ran while one was open for 4% of the time, Pallas kernels for 0%

commit v1 on v0

--- a/solution.py
+++ b/solution.py
@@ -33,7 +33,6 @@
     piece_rows = o_weight.shape[0]
     model_width = attn_out.shape[1]
     tok_count = attn_out.shape[0]
-    first_col = tower_idx % group_size * piece_rows
     routed, slot_idx = routing(modality, tower_idx, group_modality)
     group_ids = jnp.arange(NGROUP, dtype=jnp.int32)
     slot_ids = jnp.arange(CAP, dtype=jnp.int32)
@@ -47,26 +46,24 @@
     cot_send = jnp.broadcast_to(cot_group[:, None], (NGROUP, group_size, CAP, model_width)).reshape(
         tower_count, CAP, model_width
     )
-    attn_group = jnp.einsum(
-        "gct,te->gce", dispatch, attn_out, preferred_element_type=jnp.float32
-    ).astype(jnp.bfloat16)
-    attn_send = jnp.broadcast_to(
-        attn_group[:, None], (NGROUP, group_size, CAP, model_width)
-    ).reshape(tower_count, CAP, model_width)
+    attn_send = jnp.einsum(
+        "gct,tpe->gpce",
+        dispatch,
+        attn_out.reshape(tok_count, group_size, piece_rows),
+        preferred_element_type=jnp.float32,
+    ).astype(jnp.bfloat16).reshape(tower_count, CAP, piece_rows)
     attn_got = lax.all_to_all(attn_send, "tower", split_axis=0, concat_axis=0, tiled=True)
     cot_got = lax.all_to_all(cot_send, "tower", split_axis=0, concat_axis=0, tiled=True)
-    attn_use = lax.dynamic_slice_in_dim(attn_got, first_col, piece_rows, 2)
     grad_piece = lax.dot_general(
         cot_got, o_weight, (((2,), (1,)), ((), ())), preferred_element_type=jnp.float32
     ).astype(jnp.bfloat16)
     returned = lax.all_to_all(grad_piece, "tower", split_axis=0, concat_axis=0, tiled=True)
-    returned, attn_use, cot_got = (returned, attn_use, cot_got)
     returned_groups = returned.reshape(NGROUP, group_size, CAP, piece_rows)
     attn_grad = jnp.einsum(
         "gct,gpce->tpe", dispatch, returned_groups, preferred_element_type=jnp.float32
     )
     attn_grad = attn_grad.reshape(tok_count, model_width).astype(jnp.bfloat16)
-    attn_rows = attn_use.reshape(tower_count * CAP, piece_rows)
+    attn_rows = attn_got.reshape(tower_count * CAP, piece_rows)
     cot_rows = cot_got.reshape(tower_count * CAP, model_width)
     summed = lax.psum_scatter(
         lax.dot_general(

time: 402 us -> 292 us (0.73)
  waiting for transfers between devices: 278 us -> 38.7 us
  blocking collectives: 47.7 us -> 190 us
  starting transfers between devices: 21.3 us -> 11.5 us
    all_to_all x0 -> x1, blocking collectives: none -> 146 us  [per_device(): lax.all_to_all(cot_send, 'tower', split_axis=0, concat_axis=0, tiled=True)]
    all_to_all x1 -> x0, waiting for transfers between devices: 138 us -> none  [per_device(): lax.all_to_all(cot_send, 'tower', split_axis=0, concat_axis=0, tiled=True)]
    all_to_all x1, waiting for transfers between devices: 140 us -> 38.7 us  [per_device(): lax.all_to_all(attn_send, 'tower', split_axis=0, concat_axis=0, tiled=True)]
    all_to_all x1 -> x0, starting transfers between devices: 11.4 us -> none  [per_device(): lax.all_to_all(cot_send, 'tower', split_axis=0, concat_axis=0, tiled=True)]
  transfers between devices with their start and end apart: 3 -> 2, of which waited for: 2 -> 1; matrix products, arithmetic and copies ran while one was open for 4% -> 5% of each run, Pallas kernels for 0% -> 0%
where the time goes in v1:
time: 292 us; the launch traced here: 291 us
  blocking collectives  190 us (65%)
  waiting for transfers between devices  38.7 us (13%)
  matrix products  26.4 us (9%)
  between operations  14.1 us (5%)
  starting transfers between devices  11.5 us (4%)
  local copies, waits for them, and re-layouts  5.93 us (2%)
  other arithmetic  4.36 us (1%)
    all_to_all x1, blocking collectives, per_device(): lax.all_to_all(cot_send, 'tower', split_axis=0, concat_axis=0, tiled=True)  146 us
    all_to_all x1, blocking collectives, per_device(): lax.all_to_all(grad_piece, 'tower', split_axis=0, concat_axis=0, tiled=True)  44.3 us
    all_to_all x1, waiting for transfers between devices, per_device(): lax.all_to_all(attn_send, 'tower', split_axis=0, concat_axis=0, tiled=True)  38.7 us
    all_to_all x1, starting transfers between devices, per_device(): lax.all_to_all(attn_send, 'tower', split_axis=0, concat_axis=0, tiled=True)  11.4 us
    dot_general x1, matrix products, per_device(): lax.dot_general(cot_got, o_weight, (((2,), (1,)), ((), ())), preferred_el...  11 us
    dot_general x1, matrix products, per_device(): lax.dot_general(cot_rows, attn_rows, (((0,), (0,)), ((), ())), preferred_...  10.5 us
  transfers between devices with their start and end apart: 2, of which 1 were waited for; matrix products, arithmetic and copies ran while one was open for 5% of the time, Pallas kernels for 0%

profile of v1, /device:TPU:8, one launch (start us, length us, event | category | flops | bytes accessed | tf_op | source)
XLA Modules:
  0.0 291.4 jit_solution(2482524790831039994)
XLA Ops:
  7.2 0.0 copy-start
  7.2 0.7 fusion.17
  7.9 0.2 reduce_window_sum.22
  8.1 0.8 select_reduce_fusion.3
  8.9 0.7 fusion.10
  9.6 0.2 reduce_window_sum.23
  9.8 0.8 select_reduce_fusion
  10.7 0.1 and_select_fusion.1
  10.8 0.8 select_reduce_fusion.2
  11.6 2.9 %convolution_convert_fusion.1 = bf16[8,24,4,1024]{3,1,2,0:T(8,128)(2,1)} fusion(bf16[16,4,8,1024]{3,2,1,0:T(8,128)(2,1)} %bitcast.43, pred[24,128]{1,0:T(8,128)(4,1)S(1)} %iota_compare_fusion.1, pred[8,128]{1,0:T(8,128)(4,1)S(1)} %iota_compare_fusion.2), kind=kOutput, calls=%fused_computation.7 | convolution fusion | flops 202137600 | bytes 2625536 | tf_op jit(solution)/shard_map/gct,tpe->gpce/dot_general | solution.py:49
  14.5 11.4 %all-to-all-start.2 = ((bf16[32,24,1024]{2,1,0:T(8,128)(2,1)}), bf16[32,24,1024]{2,1,0:T(8,128)(2,1)}, u32[]{:S(2)}, u32[]{:S(2)}) async-start(bf16[32,24,1024]{2,1,0:T(8,128)(2,1)} %bitcast.10), calls=%async_computation.2 | async-start | bytes 3145728 | tf_op jit(solution)/shard_map/all_to_all | solution.py:55
  25.9 0.0 reduce-scatter.2.cloned.1.call-start
  26.0 0.6 convolution_convert_fusion
  26.6 38.7 %all-to-all-done.2 = bf16[32,24,1024]{2,1,0:T(8,128)(2,1)} async-done(((bf16[32,24,1024]{2,1,0:T(8,128)(2,1)}), bf16[32,24,1024]{2,1,0:T(8,128)(2,1)}, u32[]{:S(2)}, u32[]{:S(2)}) %all-to-all-start.2) | async-done | bytes 1572896 | tf_op jit(solution)/shard_map/all_to_all | solution.py:55
  65.3 0.8 broadcast_in_dim.7
  66.1 146.1 %all_to_all.15 = bf16[32,24,4096]{2,1,0:T(8,128)(2,1)S(1)} all-to-all(bf16[32,24,4096]{2,1,0:T(8,128)(2,1)S(1)} %bitcast.40), channel_id=1, replica_groups=mesh['dp'=8,'tower'=32] {'tower'}, dimensions={0} | all-to-all | bytes 12582912 | tf_op jit(solution)/shard_map/all_to_all | solution.py:56
  212.1 2.7 copy-done.1
  214.8 10.5 %bitcast_convert_fusion = bf16[4096,1024]{1,0:T(8,128)(2,1)} fusion(bf16[32,24,4096]{2,1,0:T(8,128)(2,1)S(1)} %all_to_all.15, bf16[32,24,1024]{2,1,0:T(8,128)(2,1)} %all-to-all-done.2), kind=kOutput, calls=%fused_computation | convolution fusion | flops 6446645248 | bytes 16252928 | tf_op jit(solution)/shard_map/dot_general | solution.py:69
  225.3 0.0 reduce-scatter.2.cloned.1.call-update
  225.3 11.0 %fusion.3 = bf16[32,24,1024]{2,1,0:T(8,128)(2,1)S(1)} fusion(bf16[32,24,4096]{2,1,0:T(8,128)(2,1)} %copy-done.1, bf16[1024,4096]{1,0:T(8,128)(2,1)} %param.9), kind=kOutput, calls=%fused_computation.6 | convolution fusion | flops 6443237376 | bytes 16252928 | tf_op jit(solution)/shard_map/dot_general | solution.py:57
  236.4 44.3 %all_to_all.16 = bf16[32,24,1024]{2,1,0:T(8,128)(2,1)S(1)} all-to-all(bf16[32,24,1024]{2,1,0:T(8,128)(2,1)S(1)} %fusion.3), channel_id=1, replica_groups=mesh['dp'=8,'tower'=32] {'tower'}, dimensions={0} | all-to-all | bytes 3145728 | tf_op jit(solution)/shard_map/all_to_all | solution.py:60
  280.7 0.2 copy.22
  280.8 1.5 fusion.2
  282.3 2.3 copy.19
  (5 shorter events, 0.0 us)
Async XLA Ops:
  7.2 18.8 %copy-start = (bf16[128,4096]{1,0:T(8,128)(2,1)S(1)}, bf16[128,4096]{1,0:T(8,128)(2,1)}, u32[]{:S(2)}) copy-start(bf16[128,4096]{1,0:T(8,128)(2,1)} %param.6) | copy-start | bytes 3145732
  14.5 50.8 %all-to-all-start.2 = ((bf16[32,24,1024]{2,1,0:T(8,128)(2,1)}), bf16[32,24,1024]{2,1,0:T(8,128)(2,1)}, u32[]{:S(2)}, u32[]{:S(2)}) async-start(bf16[32,24,1024]{2,1,0:T(8,128)(2,1)} %bitcast.10), calls=%async_computation.2 | async-start | bytes 3145728 | tf_op jit(solution)/shard_map/all_to_all | solution.py:55
  25.9 256.4 %reduce-scatter.2.cloned.1.call-start = ((), (), s32[]{:S(2)}) async-start(), calls=%async_computation.4 | async-start | bytes 9437184 | tf_op jit(solution)/shard_map/reduce_scatter | solution.py:68
  212.1 2.7 copy-start.1
Sparse Core Ops, SparseCore 0:
  225.5 49.0 reduce-scatter.1

commit v2 on v1

--- a/solution.py
+++ b/solution.py
@@ -1,10 +1,18 @@
+import functools
+
 import jax
 import jax.numpy as jnp
 from jax import lax
+from jax.experimental import pallas as pl
+from jax.experimental.pallas import tpu as pltpu
 from jax.sharding import PartitionSpec as P
 
 NGROUP = 8
 CAP = 24
+NX = 4
+NZ = 8
+NC = 4
+MESH = pl.DeviceIdType.MESH
 
 
 def routing(modal_rows, tower_idx, group_modality):
@@ -26,13 +34,159 @@
     return (routed, slot_idx)
 
 
+def dispatch_kernel(
+    dest_ref, cot_ref, out_ref, ring, dests, staged,
+    dest_send, dest_recv, right_send, right_recv, left_send, left_recv, x_send, x_recv, own_sem,
+):
+    width = cot_ref.shape[1] // NC
+    half = width // 2
+    me = lax.axis_index("tower")
+    my_x, my_z = me // NZ, me % NZ
+    my_half = my_z // (NZ // 2)
+
+    def at_z(z):
+        return my_x * NZ + (z + NZ) % NZ
+
+    def at_x(x):
+        return ((x + NX) % NX) * NZ + my_z
+
+    barrier = pltpu.get_barrier_semaphore()
+    for k in range(1, NZ):
+        pl.semaphore_signal(barrier, inc=1, device_id={"tower": at_z(my_z + k)}, device_id_type=MESH)
+    for k in range(1, NX):
+        pl.semaphore_signal(barrier, inc=1, device_id={"tower": at_x(my_x + k)}, device_id_type=MESH)
+    pl.semaphore_wait(barrier, NZ - 1 + NX - 1)
+
+    def dest_copy(k):
+        return pltpu.make_async_remote_copy(
+            src_ref=dest_ref,
+            dst_ref=dests.at[NZ - k],
+            send_sem=dest_send.at[k],
+            recv_sem=dest_recv.at[NZ - k],
+            device_id={"tower": at_z(my_z + k)},
+            device_id_type=MESH,
+        )
+
+    def block(c, off):
+        return cot_ref.at[:, pl.ds(c * width, width)] if off == 0 else ring.at[c, off % NZ]
+
+    def ring_copy(c, s, right):
+        off = -s if right else s
+        src = block(c, off)
+        dst = ring.at[c, (off - 1 if right else off + 1) % NZ]
+        if s == NZ // 2 - 1:
+            cols = pl.ds(0, half) if right else pl.ds(half, half)
+            src, dst = src.at[:, cols], dst.at[:, cols]
+        return pltpu.make_async_remote_copy(
+            src_ref=src,
+            dst_ref=dst,
+            send_sem=(right_send if right else left_send).at[c, s],
+            recv_sem=(right_recv if right else left_recv).at[c, s],
+            device_id={"tower": at_z(my_z + (1 if right else -1))},
+            device_id_type=MESH,
+        )
+
+    rows = lax.broadcasted_iota(jnp.int32, (NX * CAP, 128), 0)
+    x_of = sum((rows >= CAP * k).astype(jnp.int32) for k in range(1, NX))
+    wanted = rows + CAP * x_of + CAP * my_half
+
+    def deliver(c, off):
+        d = dest_ref[0:1, :] if off == 0 else dests[off % NZ, 0:1, :]
+        pick = jnp.where(wanted == d, 1.0, 0.0).astype(jnp.bfloat16)
+        got = jnp.dot(pick, block(c, off)[...], preferred_element_type=jnp.float32)
+        got = got.astype(jnp.bfloat16)
+        slot = off % NZ
+        z_from = (my_z + off + NZ) % NZ
+        for x in range(NX):
+            staged[x, c, slot] = got[x * CAP:(x + 1) * CAP]
+
+        for k in range(NX):
+            x = (my_x + k) % NX
+            src = staged.at[x, c, slot]
+            dst = out_ref.at[my_x * NZ + z_from, :, pl.ds(c * width, width)]
+            if k == 0:
+                pltpu.make_async_copy(src, dst, own_sem).start()
+            else:
+                pltpu.make_async_remote_copy(
+                    src_ref=src, dst_ref=dst, send_sem=x_send.at[k], recv_sem=x_recv.at[NX - k],
+                    device_id={"tower": at_x(my_x + k)}, device_id_type=MESH,
+                ).start()
+
+    for k in range(1, NZ):
+        dest_copy(k).start()
+
+    for c0 in range(0, NC, 2):
+        for s in range(NZ // 2):
+            for c in (c0, c0 + 1):
+                if s > 0:
+                    ring_copy(c, s - 1, True).wait_recv()
+                    ring_copy(c, s - 1, False).wait_recv()
+                ring_copy(c, s, True).start()
+                ring_copy(c, s, False).start()
+                if c == 0 and s == 0:
+                    for k in range(1, NZ):
+                        dest_copy(k).wait_recv()
+                if s == 0:
+                    deliver(c, 0)
+                else:
+                    deliver(c, -s)
+                    deliver(c, s)
+        for c in (c0, c0 + 1):
+            ring_copy(c, NZ // 2 - 1, True).wait_recv()
+            ring_copy(c, NZ // 2 - 1, False).wait_recv()
+            deliver(c, NZ // 2)
+
+    for k in range(1, NZ):
+        dest_copy(k).wait_send()
+    for c in range(NC):
+        for s in range(NZ // 2):
+            ring_copy(c, s, True).wait_send()
+            ring_copy(c, s, False).wait_send()
+    for k in range(NX):
+        x = (my_x + k) % NX
+        src = staged.at[x]
+        if k == 0:
+            pltpu.make_async_copy(src, src, own_sem).wait()
+        else:
+            pltpu.make_async_copy(src, src, x_send.at[k]).wait()
+            pltpu.make_async_copy(src, src, x_recv.at[k]).wait()
+
+
+def dispatch_cot(dest, cot):
+    tok, width = cot.shape[0], cot.shape[1] // NC
+    return pl.pallas_call(
+        dispatch_kernel,
+        out_shape=jax.ShapeDtypeStruct((NX * NZ, CAP, NC * width), jnp.bfloat16),
+        in_specs=[pl.BlockSpec(memory_space=pltpu.VMEM)] * 2,
+        out_specs=pl.BlockSpec(memory_space=pl.ANY),
+        scratch_shapes=[
+            pltpu.VMEM((NC, NZ, tok, width), jnp.bfloat16),
+            pltpu.VMEM((NZ, 8, 128), jnp.int32),
+            pltpu.VMEM((NX, NC, NZ, CAP, width), jnp.bfloat16),
+            pltpu.SemaphoreType.DMA((NZ,)),
+            pltpu.SemaphoreType.DMA((NZ,)),
+            pltpu.SemaphoreType.DMA((NC, NZ // 2)),
+            pltpu.SemaphoreType.DMA((NC, NZ // 2)),
+            pltpu.SemaphoreType.DMA((NC, NZ // 2)),
+            pltpu.SemaphoreType.DMA((NC, NZ // 2)),
+            pltpu.SemaphoreType.DMA((NX,)),
+            pltpu.SemaphoreType.DMA((NX,)),
+            pltpu.SemaphoreType.DMA,
+        ],
+        compiler_params=pltpu.CompilerParams(
+            collective_id=0, has_side_effects=True, vmem_limit_bytes=40 * 1024 * 1024
+        ),
+        cost_estimate=pl.CostEstimate(flops=6_000_000_000, bytes_accessed=250_000_000, transcendentals=0),
+        name="dispatch_cot",
+    )(dest, cot)
+
+
 def per_device(attn_out, out_cot, modality, group_modality, o_weight):
     tower_idx = lax.axis_index("tower")
     tower_count = lax.axis_size("tower")
     group_size = tower_count // NGROUP
     piece_rows = o_weight.shape[0]
-    model_width = attn_out.shape[1]
-    tok_count = attn_out.shape[0]
+    tok_count, model_width = attn_out.shape
     routed, slot_idx = routing(modality, tower_idx, group_modality)
     group_ids = jnp.arange(NGROUP, dtype=jnp.int32)
     slot_ids = jnp.arange(CAP, dtype=jnp.int32)
@@ -40,12 +194,6 @@
         (routed[None, None, :] == group_ids[:, None, None])
         & (slot_idx[None, None, :] == slot_ids[None, :, None])
     ).astype(jnp.bfloat16)
-    cot_group = jnp.einsum(
-        "gct,te->gce", dispatch, out_cot, preferred_element_type=jnp.float32
-    ).astype(jnp.bfloat16)
-    cot_send = jnp.broadcast_to(cot_group[:, None], (NGROUP, group_size, CAP, model_width)).reshape(
-        tower_count, CAP, model_width
-    )
     attn_send = jnp.einsum(
         "gct,tpe->gpce",
         dispatch,
@@ -53,7 +201,10 @@
         preferred_element_type=jnp.float32,
     ).astype(jnp.bfloat16).reshape(tower_count, CAP, piece_rows)
     attn_got = lax.all_to_all(attn_send, "tower", split_axis=0, concat_axis=0, tiled=True)
-    cot_got = lax.all_to_all(cot_send, "tower", split_axis=0, concat_axis=0, tiled=True)
+
+    dest = jnp.broadcast_to((routed * CAP + slot_idx)[None, :], (8, tok_count))
+    cot_got = dispatch_cot(dest, out_cot)
+
     grad_piece = lax.dot_general(
         cot_got, o_weight, (((2,), (1,)), ((), ())), preferred_element_type=jnp.float32
     ).astype(jnp.bfloat16)
@@ -72,8 +223,8 @@
         "dp",
         scatter_dimension=0,
         tiled=True,
-    ).astype(jnp.float32)
-    weight_grad = summed.T.astype(jnp.bfloat16)
+    )
+    weight_grad = summed.T
     return (attn_grad, weight_grad)
 
 

time: 292 us -> 234 us (0.80)
  blocking collectives: 190 us -> 46.3 us
  Pallas kernels: 0 us -> 125 us
  waiting for transfers between devices: 38.7 us -> 0.02 us
    all_to_all x1 -> x0, blocking collectives: 146 us -> none  [per_device(): lax.all_to_all(cot_send, 'tower', split_axis=0, concat_axis=0, tiled=True)]
    pallas_call x0 -> x1, Pallas kernels: none -> 125 us  [dispatch_cot(): pl.pallas_call(dispatch_kernel, out_shape=jax.ShapeDtypeStruct((NX * NZ,...]
    all_to_all x1, waiting for transfers between devices: 38.7 us -> 0.01 us  [per_device(): lax.all_to_all(attn_send, 'tower', split_axis=0, concat_axis=0, tiled=True)]
  transfers between devices with their start and end apart: 2 -> 2, of which waited for: 1 -> 0; matrix products, arithmetic and copies ran while one was open for 5% -> 5% of each run, Pallas kernels for 0% -> 54%
where the time goes in v2:
time: 234 us
  Pallas kernels  125 us (53%)
  blocking collectives  46.3 us (20%)
  matrix products  27.3 us (12%)
  between operations  14.1 us (6%)
  starting transfers between devices  11.4 us (5%)
  local copies, waits for them, and re-layouts  5.15 us (2%)
  other arithmetic  4.48 us (2%)
    pallas_call x1, Pallas kernels, dispatch_cot(): pl.pallas_call(dispatch_kernel, out_shape=jax.ShapeDtypeStruct((NX * NZ,...  125 us
    all_to_all x1, blocking collectives, per_device(): lax.all_to_all(grad_piece, 'tower', split_axis=0, concat_axis=0, tiled=True)  46.3 us
    dot_general x1, matrix products, per_device(): lax.dot_general(cot_rows, attn_rows, (((0,), (0,)), ((), ())), preferred_...  11.9 us
    all_to_all x1, starting transfers between devices, per_device(): lax.all_to_all(attn_send, 'tower', split_axis=0, concat_axis=0, tiled=True)  11.3 us
    dot_general x1, matrix products, per_device(): lax.dot_general(cot_got, o_weight, (((2,), (1,)), ((), ())), preferred_el...  11 us
    unnamed x5, local copies, waits for them, and re-layouts  4.98 us
  transfers between devices with their start and end apart: 2, of which 0 were waited for; matrix products, arithmetic and copies ran while one was open for 5% of the time, Pallas kernels for 54%

profile of v2, /device:TPU:8, one launch (start us, length us, event | category | flops | bytes accessed | tf_op | source)
XLA Modules:
  0.0 233.9 jit_solution(1794186806058667817)
XLA Ops:
  7.2 0.0 copy-start
  7.2 0.7 fusion.13
  7.9 0.2 reduce_window_sum.22
  8.1 0.8 select_reduce_fusion.3
  8.9 0.7 fusion.8
  9.6 0.2 reduce_window_sum.23
  9.8 0.8 select_reduce_fusion
  10.6 0.1 and_select_fusion.1
  10.8 0.8 select_reduce_fusion.2
  11.5 0.1 multiply_add_fusion
  11.7 2.9 %convolution_convert_fusion = bf16[8,24,4,1024]{3,1,2,0:T(8,128)(2,1)} fusion(bf16[16,4,8,1024]{3,2,1,0:T(8,128)(2,1)} %bitcast.38, pred[24,128]{1,0:T(8,128)(4,1)S(1)} %iota_compare_fusion.1, pred[8,128]{1,0:T(8,128)(4,1)S(1)} %iota_compare_fusion.2), kind=kOutput, calls=%fused_computation.6 | convolution fusion | flops 202137600 | bytes 2625536 | tf_op jit(solution)/shard_map/gct,tpe->gpce/dot_general | solution.py:197
  14.6 11.3 %all-to-all-start.1 = ((bf16[32,24,1024]{2,1,0:T(8,128)(2,1)}), bf16[32,24,1024]{2,1,0:T(8,128)(2,1)S(1)}, u32[]{:S(2)}, u32[]{:S(2)}) async-start(bf16[32,24,1024]{2,1,0:T(8,128)(2,1)} %bitcast.8), calls=%async_computation.1 | async-start | bytes 3145728 | tf_op jit(solution)/shard_map/all_to_all | solution.py:203
  26.0 0.0 reduce-scatter.2.cloned.1.call-start
  26.0 0.0 copy-done
  26.0 125.2 %dispatch_cot.1 = bf16[32,24,4096]{2,1,0:T(8,128)(2,1)S(1)} custom-call(s32[8,128]{1,0:T(8,128)S(1)} %broadcast_in_dim.7.dest_ref, bf16[128,4096]{1,0:T(8,128)(2,1)S(1)} %copy-done), custom_call_target="tpu_custom_call" | custom-call | flops 6000000000 | bytes 250000000 | tf_op jit(solution)/shard_map/dispatch_cot/pallas_call | solution.py:157
  151.3 2.7 %copy-done.1 = bf16[32,24,4096]{2,1,0:T(8,128)(2,1)} copy-done((bf16[32,24,4096]{2,1,0:T(8,128)(2,1)}, bf16[32,24,4096]{2,1,0:T(8,128)(2,1)S(1)}, u32[]{:S(2)}) %copy-start.1) | copy-done | bytes 6291480
  154.0 0.0 all-to-all-done.1
  154.0 11.9 %bitcast_convert_fusion = bf16[4096,1024]{1,0:T(8,128)(2,1)} fusion(bf16[32,24,4096]{2,1,0:T(8,128)(2,1)} %copy-done.1, bf16[32,24,1024]{2,1,0:T(8,128)(2,1)S(1)} %all-to-all-done.1), kind=kOutput, calls=%fused_computation | convolution fusion | flops 6446645248 | bytes 16252928 | tf_op jit(solution)/shard_map/dot_general | solution.py:220
  165.8 0.0 reduce-scatter.2.cloned.1.call-update
  165.9 11.0 %fusion.3 = bf16[32,24,1024]{2,1,0:T(8,128)(2,1)S(1)} fusion(bf16[32,24,4096]{2,1,0:T(8,128)(2,1)} %copy-done.1, bf16[1024,4096]{1,0:T(8,128)(2,1)} %param.9), kind=kOutput, calls=%fused_computation.5 | convolution fusion | flops 6443237376 | bytes 16252928 | tf_op jit(solution)/shard_map/dot_general | solution.py:208
  176.9 46.3 %all_to_all.10 = bf16[32,24,1024]{2,1,0:T(8,128)(2,1)S(1)} all-to-all(bf16[32,24,1024]{2,1,0:T(8,128)(2,1)S(1)} %fusion.3), channel_id=1, replica_groups=mesh['dp'=8,'tower'=32] {'tower'}, dimensions={0} | all-to-all | bytes 3145728 | tf_op jit(solution)/shard_map/all_to_all | solution.py:211
  223.2 0.2 copy.22
  223.4 1.5 fusion.2
  224.8 2.3 copy.19
  (5 shorter events, 0.0 us)
Async XLA Ops:
  7.2 18.9 %copy-start = (bf16[128,4096]{1,0:T(8,128)(2,1)S(1)}, bf16[128,4096]{1,0:T(8,128)(2,1)}, u32[]{:S(2)}) copy-start(bf16[128,4096]{1,0:T(8,128)(2,1)} %cot_ref.1) | copy-start | bytes 3145732
  14.6 139.3 %all-to-all-start.1 = ((bf16[32,24,1024]{2,1,0:T(8,128)(2,1)}), bf16[32,24,1024]{2,1,0:T(8,128)(2,1)S(1)}, u32[]{:S(2)}, u32[]{:S(2)}) async-start(bf16[32,24,1024]{2,1,0:T(8,128)(2,1)} %bitcast.8), calls=%async_computation.1 | async-start | bytes 3145728 | tf_op jit(solution)/shard_map/all_to_all | solution.py:203
  26.0 198.9 %reduce-scatter.2.cloned.1.call-start = ((), (), s32[]{:S(2)}) async-start(), calls=%async_computation.3 | async-start | bytes 9437184 | tf_op jit(solution)/shard_map/reduce_scatter | solution.py:219
  151.3 2.7 %copy-start.1 = (bf16[32,24,4096]{2,1,0:T(8,128)(2,1)}, bf16[32,24,4096]{2,1,0:T(8,128)(2,1)S(1)}, u32[]{:S(2)}) copy-start(bf16[32,24,4096]{2,1,0:T(8,128)(2,1)S(1)} %dispatch_cot.1) | copy-start | bytes 18874372
Sparse Core Ops, SparseCore 0:
  166.0 51.3 reduce-scatter.1

commit v3 on v1

v3 whole, which is shorter than its diff:
```python
import jax
import jax.numpy as jnp
from jax import lax
from jax.experimental import pallas as pl
from jax.experimental.pallas import tpu as pltpu
from jax.sharding import PartitionSpec as P

NGROUP = 8
CAP = 24
NX = 4
NZ = 8
HALVES = NGROUP // NX
PIECES = NZ // HALVES
NDP = 8
NC = 4
LAST = NZ // 2
TILE = 256
MESH = pl.DeviceIdType.MESH
F32 = jnp.float32
BF16 = jnp.bfloat16


def kernel(
    mod_ref, gm_ref, attn_ref, cot_ref, w_ref, grad_ref, wgrad_ref,
    ring, dests, staged, cot_got, w_chunk, partial, terms, acc,
    attn_own, attn_x, attn_got, attn_t, grads, ret_z, ret_x,
    dest_send, dest_recv, right_send, right_recv, left_send, left_recv,
    x_send, x_recv, x_own, ax_send, ax_recv, ax_own, az_send, az_recv, az_own,
    w_sem, rs_send, rs_recv, rs_own, rz_send, rz_recv, rz_own, rx_send, rx_recv, rx_own,
):
    tok = cot_ref.shape[0]
    width = cot_ref.shape[1] // NC
    cols = width // NDP
    own_cols = wgrad_ref.shape[1]
    feats = w_ref.shape[0]
    half = width // 2
    me, my_d = lax.axis_index("tower"), lax.axis_index("dp")
    my_x, my_z = me // NZ, me % NZ
    my_half, my_piece = my_z // PIECES, my_z % PIECES

    def at_z(k):
        return {"tower": my_x * NZ + (my_z + k + NZ) % NZ}

    def at_x(k):
        return {"tower": ((my_x + k) % NX) * NZ + my_z}

    def at_d(k):
        return {"dp": (my_d + k) % NDP}

    def remote(src, dst, send, recv, device):
        return pltpu.make_async_remote_copy(
            src_ref=src, dst_ref=dst, send_sem=send, recv_sem=recv,
            device_id=device, device_id_type=MESH,
        )

    def wait_bytes(ref, sem):
        pltpu.make_async_copy(ref, ref, sem).wait()

    def w_load(c, d):
        return pltpu.make_async_copy(
            w_ref.at[:, pl.ds(d * own_cols + c * cols, cols)],
            w_chunk.at[c % 2, :, pl.ds(d * cols, cols)],
            w_sem.at[c],
        )

    barrier = pltpu.get_barrier_semaphore()
    for k in range(1, NZ):
        pl.semaphore_signal(barrier, inc=1, device_id=at_z(k), device_id_type=MESH)
    for k in range(1, NX):
        pl.semaphore_signal(barrier, inc=1, device_id=at_x(k), device_id_type=MESH)
    for k in range(1, NDP):
        pl.semaphore_signal(barrier, inc=1, device_id=at_d(k), device_id_type=MESH)

    for c in range(NC):
        for d in range(NDP):
            ring[c, 0, :, d * cols:(d + 1) * cols] = cot_ref[
                :, d * own_cols + c * cols:d * own_cols + (c + 1) * cols
            ]
    for c in range(2):
        for d in range(NDP):
            w_load(c, d).start()
    pl.semaphore_wait(barrier, NZ - 1 + NX - 1 + NDP - 1)

    def ring_copy(c, s, right):
        off = -s if right else s
        src = ring.at[c, off % NZ]
        dst = ring.at[c, (off - 1 if right else off + 1) % NZ]
        if s == LAST - 1:
            part = pl.ds(0, half) if right else pl.ds(half, half)
            src, dst = src.at[:, part], dst.at[:, part]
        return remote(
            src, dst,
            (right_send if right else left_send).at[c, s],
            (right_recv if right else left_recv).at[c, s],
            at_z(1 if right else -1),
        )

    ring_copy(0, 0, True).start()
    ring_copy(0, 0, False).start()

    mod = jnp.broadcast_to(mod_ref[...], (8, tok))
    kinds = [(mod == m).astype(F32) for m in range(3)]
    t_from = lax.broadcasted_iota(jnp.int32, (tok, tok), 0)
    t_to = lax.broadcasted_iota(jnp.int32, (tok, tok), 1)
    earlier = (t_from < t_to).astype(F32).astype(BF16)
    before = jnp.dot(jnp.concatenate(kinds, 0).astype(BF16), earlier, preferred_element_type=F32)
    order = sum(before[8 * m:8 * m + 8] * kinds[m] for m in range(3))
    serves = [gm_ref[g] for g in range(NGROUP)]
    how_many = jnp.ones_like(mod)
    for m in range(3):
        count = sum((s == m).astype(jnp.int32) for s in serves)
        how_many = jnp.where(mod == m, count, how_many)
    per = how_many.astype(F32)
    turn = (order.astype(jnp.int32) + me).astype(F32)
    target = (turn - jnp.floor((turn + 0.5) / per) * per).astype(jnp.int32)
    routed = jnp.zeros_like(mod)
    for g in range(NGROUP):
        rank = sum(((s == serves[g]).astype(jnp.int32) for s in serves[:g]), jnp.int32(0))
        routed = jnp.where((mod == serves[g]) & (target == rank), g, routed)
    dest = routed * CAP + jnp.floor((order + 0.5) / per).astype(jnp.int32)
    dests[0] = dest

    def dest_copy(k):
        return remote(dests.at[0], dests.at[NZ - k], dest_send.at[k], dest_recv.at[NZ - k], at_z(k))

    for k in range(1, NZ):
        dest_copy(k).start()

    slots = lax.broadcasted_iota(jnp.int32, (NGROUP * CAP, tok), 0)
    pick_own = jnp.where(slots == dest[0:1], 1.0, 0.0).astype(BF16)
    for p in range(PIECES):
        got = jnp.dot(pick_own, attn_ref[:, p * feats:(p + 1) * feats], preferred_element_type=F32)
        attn_own[:, :, :, p * feats:(p + 1) * feats] = got.astype(BF16).reshape(NX, HALVES, CAP, feats)

    def attn_x_copy(k):
        return remote(
            attn_own.at[(my_x + k) % NX], attn_x.at[my_x], ax_send.at[k], ax_recv.at[NX - k], at_x(k)
        )

    own_ax = pltpu.make_async_copy(attn_own.at[my_x], attn_x.at[my_x], ax_own)
    own_ax.start()
    for k in range(1, NX):
        attn_x_copy(k).start()

    def attn_z_src(k):
        z = (my_z + k) % NZ
        start = pl.multiple_of((z % PIECES) * feats, feats)
        return attn_x.at[:, z // PIECES, :, pl.ds(start, feats)]

    def attn_z_copy(k):
        return remote(
            attn_z_src(k), attn_got.at[:, my_z], az_send.at[k], az_recv.at[NZ - k], at_z(k)
        )

    def attn_along_z():
        own_ax.wait()
        for k in range(1, NX):
            attn_x_copy(k).wait_recv()
        pltpu.make_async_copy(attn_z_src(0), attn_got.at[:, my_z], az_own).start()
        for k in range(1, NZ):
            attn_z_copy(k).start()

    def attn_arrived():
        pltpu.make_async_copy(attn_z_src(0), attn_got.at[:, my_z], az_own).wait()
        for k in range(1, NZ):
            attn_z_copy(k).wait_recv()

        @pl.loop(0, feats // TILE)
        def _(j):
            at = pl.ds(pl.multiple_of(j * TILE, TILE), TILE)
            attn_t[at, :] = jnp.transpose(attn_got[:, :, :, at].reshape(NX * NZ * CAP, TILE))

    rows = lax.broadcasted_iota(jnp.int32, (NX * CAP, tok), 0)
    x_of = sum((rows >= CAP * k).astype(jnp.int32) for k in range(1, NX))
    wanted = rows + CAP * (HALVES - 1) * x_of + CAP * my_half

    def deliver(c, off):
        slot = off % NZ
        pick = jnp.where(wanted == dests[slot, 0:1, :], 1.0, 0.0).astype(BF16)
        got = jnp.dot(pick, ring[c, slot], preferred_element_type=F32).astype(BF16)
        for x in range(NX):
            staged[c % 2, x, slot] = got[x * CAP:(x + 1) * CAP]
        lands = cot_got.at[c, my_x, (my_z + off + NZ) % NZ]
        for k in range(NX):
            src = staged.at[c % 2, (my_x + k) % NX, slot]
            if k == 0:
                pltpu.make_async_copy(src, lands, x_own.at[c]).start()
            else:
                remote(src, lands, x_send.at[c, k], x_recv.at[c, NX - k], at_x(k)).start()

    def chunk_arrived(c):
        wait_bytes(staged.at[c % 2, 0], x_own.at[c])
        for k in range(1, NX):
            wait_bytes(staged.at[c % 2, k], x_recv.at[c, k])

    def x_sends_done(c):
        for k in range(1, NX):
            wait_bytes(staged.at[c % 2, k], x_send.at[c, k])

    def input_grad(c):
        wait_bytes(w_chunk.at[c % 2], w_sem.at[c])

        @pl.loop(0, feats // TILE)
        def _(j):
            at = pl.ds(pl.multiple_of(j * TILE, TILE), TILE)
            term = lax.dot_general(
                cot_got[c].reshape(NX * NZ * CAP, width), w_chunk[c % 2, at, :],
                (((1,), (1,)), ((), ())), preferred_element_type=F32,
            )
            if c > 0:
                term += acc[:, at]
            if c < NC - 1:
                acc[:, at] = term
            else:
                grads[:, :, :, at] = term.astype(BF16).reshape(NX, NZ, CAP, TILE)

        if c + 2 < NC:
            for d in range(NDP):
                w_load(c + 2, d).start()

    def rs_copy(c, k):
        return remote(
            partial.at[c % 2, (my_d + k) % NDP], terms.at[c, my_d],
            rs_send.at[c, k], rs_recv.at[c, NDP - k], at_d(k),
        )

    def rs_own_copy(c):
        return pltpu.make_async_copy(partial.at[c % 2, my_d], terms.at[c, my_d], rs_own.at[c])

    def weight_grad(c):
        if c >= 2:
            for k in range(1, NDP):
                rs_copy(c - 2, k).wait_send()
            rs_own_copy(c - 2).wait()

        per_tile = TILE // cols

        @pl.loop(0, width // TILE)
        def _(j):
            at = pl.ds(pl.multiple_of(j * TILE, TILE), TILE)
            term = jnp.dot(
                attn_t[...], cot_got[c, :, :, :, at].reshape(NX * NZ * CAP, TILE),
                preferred_element_type=F32,
            ).astype(BF16)
            for i in range(per_tile):
                partial[c % 2, j * per_tile + i] = term[:, i * cols:(i + 1) * cols]

        rs_own_copy(c).start()
        for k in range(1, NDP):
            rs_copy(c, k).start()

    def weight_grad_sum(c):
        if c >= NC - 2:
            rs_own_copy(c).wait()
        for k in range(1, NDP):
            rs_copy(c, k).wait_recv()

        @pl.loop(0, feats // TILE)
        def _(j):
            at = pl.ds(pl.multiple_of(j * TILE, TILE), TILE)
            total = terms[c, 0, at, :].astype(F32)
            for d in range(1, NDP):
                total += terms[c, d, at, :].astype(F32)
            wgrad_ref[at, c * cols:(c + 1) * cols] = total.astype(BF16)

    def ret_z_copy(k):
        return remote(
            grads.at[:, (my_z + k) % NZ], ret_z.at[my_z], rz_send.at[k], rz_recv.at[NZ - k], at_z(k)
        )

    for tick in range(2 * NC + LAST):
        live = [(c, tick - 2 * c) for c in range(NC) if 0 <= tick - 2 * c < 8]
        for c, s in live:
            if s in range(1, LAST + 1):
                ring_copy(c, s - 1, True).wait_recv()
                ring_copy(c, s - 1, False).wait_recv()
            if s < LAST and (c, s) != (0, 0):
                ring_copy(c, s, True).start()
                ring_copy(c, s, False).start()
        if tick == 1:
            for k in range(1, NZ):
                dest_copy(k).wait_recv()
        if tick == 2:
            attn_along_z()
        for c, s in live:
            if s == 0:
                if c < 2:
                    deliver(c, 0)
            elif s < LAST:
                if s == 1 and c >= 2:
                    x_sends_done(c - 2)
                    deliver(c, 0)
                deliver(c, -s)
                deliver(c, s)
            elif s == LAST:
                deliver(c, LAST)
            elif s == LAST + 1:
                chunk_arrived(c)
                if c == 0:
                    attn_arrived()
                input_grad(c)
                if c == NC - 1:
                    pltpu.make_async_copy(grads.at[:, my_z], ret_z.at[my_z], rz_own).start()
                    for k in range(1, NZ):
                        ret_z_copy(k).start()
                weight_grad(c)
                if c == 2:
                    weight_grad_sum(0)

    for c in range(1, NC - 1):
        weight_grad_sum(c)

    def ret_x_start(z):
        for k in range(NX):
            src, dst = ret_z.at[z, (my_x + k) % NX], ret_x.at[my_x, z]
            if k == 0:
                pltpu.make_async_copy(src, dst, rx_own).start()
            else:
                remote(src, dst, rx_send.at[k], rx_recv.at[NX - k], at_x(k)).start()

    pltpu.make_async_copy(grads.at[:, my_z], ret_z.at[my_z], rz_own).wait()
    ret_x_start(my_z)
    for k in (1, 7, 2, 6, 3, 5, 4):
        ret_z_copy(k).wait_recv()
        ret_x_start((my_z - k + NZ) % NZ)
    weight_grad_sum(NC - 1)
    for k in range(NX):
        wait_bytes(ret_x.at[k], rx_own if k == 0 else rx_recv.at[k])

    back = jnp.where(slots == dests[0, 0:1, :], 1.0, 0.0).astype(BF16)
    for p in range(PIECES):
        pieces = jnp.concatenate(
            [ret_x[g // HALVES, (g % HALVES) * PIECES + p] for g in range(NGROUP)], 0
        )
        grad_ref[:, p * feats:(p + 1) * feats] = lax.dot_general(
            back, pieces, (((0,), (0,)), ((), ())), preferred_element_type=F32
        ).astype(BF16)

    for k in range(1, NZ):
        dest_copy(k).wait_send()
        attn_z_copy(k).wait_send()
        ret_z_copy(k).wait_send()
    for k in range(1, NX):
        attn_x_copy(k).wait_send()
        wait_bytes(ret_x.at[k], rx_send.at[k])
    for c in range(NC):
        for s in range(LAST):
            ring_copy(c, s, True).wait_send()
            ring_copy(c, s, False).wait_send()
    for c in range(NC - 2, NC):
        x_sends_done(c)
        for k in range(1, NDP):
            rs_copy(c, k).wait_send()


def backward(mod, gm, attn, cot, w):
    tok, model = cot.shape
    width = model // NC
    feats = w.shape[0]
    dma = pltpu.SemaphoreType.DMA
    vmem = pl.BlockSpec(memory_space=pltpu.VMEM)
    return pl.pallas_call(
        kernel,
        out_shape=(
            jax.ShapeDtypeStruct((tok, model), BF16),
            jax.ShapeDtypeStruct((feats, model // NDP), BF16),
        ),
        in_specs=[
            vmem, pl.BlockSpec(memory_space=pltpu.SMEM), vmem, vmem,
            pl.BlockSpec(memory_space=pl.ANY),
        ],
        out_specs=(vmem, vmem),
        scratch_shapes=[
            pltpu.VMEM((NC, NZ, tok, width), BF16),
            pltpu.VMEM((NZ, 8, tok), jnp.int32),
            pltpu.VMEM((2, NX, NZ, CAP, width), BF16),
            pltpu.VMEM((NC, NX, NZ, CAP, width), BF16),
            pltpu.VMEM((2, feats, width), BF16),
            pltpu.VMEM((2, NDP, feats, width // NDP), BF16),
            pltpu.VMEM((NC, NDP, feats, width // NDP), BF16),
            pltpu.VMEM((NX * NZ * CAP, feats), F32),
            pltpu.VMEM((NX, HALVES, CAP, model), BF16),
            pltpu.VMEM((NX, HALVES, CAP, model), BF16),
            pltpu.VMEM((NX, NZ, CAP, feats), BF16),
            pltpu.VMEM((feats, NX * NZ * CAP), BF16),
            pltpu.VMEM((NX, NZ, CAP, feats), BF16),
            pltpu.VMEM((NZ, NX, CAP, feats), BF16),
            pltpu.VMEM((NX, NZ, CAP, feats), BF16),
            dma((NZ,)), dma((NZ,)),
            dma((NC, LAST)), dma((NC, LAST)), dma((NC, LAST)), dma((NC, LAST)),
            dma((NC, NX)), dma((NC, NX)), dma((NC,)),
            dma((NX,)), dma((NX,)), dma,
            dma((NZ,)), dma((NZ,)), dma,
            dma((NC,)),
            dma((NC, NDP)), dma((NC, NDP)), dma((NC,)),
            dma((NZ,)), dma((NZ,)), dma,
            dma((NX,)), dma((NX,)), dma,
        ],
        compiler_params=pltpu.CompilerParams(
            collective_id=0, has_side_effects=True, vmem_limit_bytes=63 * 1024 * 1024
        ),
        name="moe_proj_backward",
    )(mod, gm, attn, cot, w)


def per_device(attn_out, out_cot, modality, group_modality, o_weight):
    return backward(modality.reshape(1, -1), group_modality, attn_out, out_cot, o_weight)


def solution(mesh):
    return jax.shard_map(
        per_device,
        mesh=mesh,
        in_specs=(
            P(("dp", "tower"), None),
            P(("dp", "tower"), None),
            P(("dp", "tower")),
            P(),
            P("tower", None),
        ),
        out_specs=(P(("dp", "tower"), None), P("tower", "dp")),
        check_vma=False,
    )
```

time: 292 us -> 198 us (0.68)
  Pallas kernels: 0 us -> 192 us
  blocking collectives: 190 us -> 0 us
  waiting for transfers between devices: 38.7 us -> 0 us
  matrix products: 26.4 us -> 0 us
  between operations: 14.1 us -> 0.64 us
  starting transfers between devices: 11.5 us -> 0 us
  other arithmetic: 4.36 us -> 0 us
    pallas_call x0 -> x1, Pallas kernels: none -> 192 us  [backward(): pl.pallas_call(kernel, out_shape=(jax.ShapeDtypeStruct((tok, model), BF16...]
    all_to_all x2 -> x0, blocking collectives: 190 us -> none  [the longest x1 146 us: per_device(): lax.all_to_all(cot_send, 'tower', split_axis=0, concat_axis=0, tiled=True)]
    all_to_all x1 -> x0, waiting for transfers between devices: 38.7 us -> none  [per_device(): lax.all_to_all(attn_send, 'tower', split_axis=0, concat_axis=0, tiled=True)]
    dot_general x5 -> x0, matrix products: 26.4 us -> none  [the longest x1 11 us: per_device(): lax.dot_general(cot_got, o_weight, (((2,), (1,)), ((), ())), preferred_el...]
    all_to_all x1 -> x0, starting transfers between devices: 11.4 us -> none  [per_device(): lax.all_to_all(attn_send, 'tower', split_axis=0, concat_axis=0, tiled=True)]
  transfers between devices with their start and end apart: 2 -> 0, of which waited for: 1 -> 0; matrix products, arithmetic and copies ran while one was open for 5% -> 0% of each run, Pallas kernels for 0% -> 0%
where the time goes in v3:
time: 198 us; the launch traced here: 197 us
  Pallas kernels  192 us (97%)
  local copies, waits for them, and re-layouts  4.55 us (2%)
    pallas_call x1, Pallas kernels, backward(): pl.pallas_call(kernel, out_shape=(jax.ShapeDtypeStruct((tok, model), BF16...  192 us
    unnamed x2, local copies, waits for them, and re-layouts  4.55 us

profile of v3, /device:TPU:8, one launch (start us, length us, event | category | flops | bytes accessed | tf_op | source)
XLA Modules:
  0.0 196.7 jit_solution(2687785377820220362)
XLA Ops:
  0.6 191.5 %moe_proj_backward.1 = (bf16[128,4096]{1,0:T(8,128)(2,1)}, bf16[1024,512]{1,0:T(8,128)(2,1)}) custom-call(s32[1,128]{1,0:T(1,128)} %bitcast.1, s32[8]{0:T(128)} %gm_ref.1, bf16[128,4096]{1,0:T(8,128)(2,1)} %attn_ref.1, bf16[128,4096]{1,0:T(8,128)(2,1)} %cot_ref.1, bf16[1024,4096]{1,0:T(8,128)(2,1)} %w_ref.1), custom_call_target="tpu_custom_call" | custom-call | tf_op jit(solution)/shard_map/moe_proj_backward/pallas_call | solution.py:362
  192.2 2.3 %copy.9 = bf16[128,4096]{1,0:T(8,128)(2,1)} copy(bf16[128,4096]{1,0:T(8,128)(2,1)} %get-tuple-element.4) | data formatting | bytes 2097152
  194.5 2.3 %copy.10 = bf16[1024,512]{1,0:T(8,128)(2,1)} copy(bf16[1024,512]{1,0:T(8,128)(2,1)} %get-tuple-element.5) | data formatting | bytes 2097152

commit v4 on v3

--- a/solution.py
+++ b/solution.py
@@ -12,6 +12,8 @@
 HALVES = NGROUP // NX
 PIECES = NZ // HALVES
 NDP = 8
+CORES = 2
+NY = NDP // CORES
 NC = 4
 LAST = NZ // 2
 TILE = 256
@@ -22,11 +24,11 @@
 
 def kernel(
     mod_ref, gm_ref, attn_ref, cot_ref, w_ref, grad_ref, wgrad_ref,
-    ring, dests, staged, cot_got, w_chunk, partial, terms, acc,
+    ring, dests, staged, cot_got, w_chunk, partial, other, terms, acc,
     attn_own, attn_x, attn_got, attn_t, grads, ret_z, ret_x,
     dest_send, dest_recv, right_send, right_recv, left_send, left_recv,
     x_send, x_recv, x_own, ax_send, ax_recv, ax_own, az_send, az_recv, az_own,
-    w_sem, rs_send, rs_recv, rs_own, rz_send, rz_recv, rz_own, rx_send, rx_recv, rx_own,
+    w_sem, pair_send, pair_recv, rs_send, rs_recv, rs_own, rz_send, rz_recv, rz_own, rx_send, rx_recv, rx_own,
 ):
     tok = cot_ref.shape[0]
     width = cot_ref.shape[1] // NC
@@ -36,7 +38,8 @@
     half = width // 2
     me, my_d = lax.axis_index("tower"), lax.axis_index("dp")
     my_x, my_z = me // NZ, me % NZ
-    my_half, my_piece = my_z // PIECES, my_z % PIECES
+    my_half = my_z // PIECES
+    my_y, my_core = my_d // CORES, my_d % CORES
 
     def at_z(k):
         return {"tower": my_x * NZ + (my_z + k + NZ) % NZ}
@@ -44,8 +47,10 @@
     def at_x(k):
         return {"tower": ((my_x + k) % NX) * NZ + my_z}
 
-    def at_d(k):
-        return {"dp": (my_d + k) % NDP}
+    def at_y(k):
+        return {"dp": ((my_y + k) % NY) * CORES + my_core}
+
+    other_core = {"dp": my_y * CORES + 1 - my_core}
 
     def remote(src, dst, send, recv, device):
         return pltpu.make_async_remote_copy(
@@ -68,18 +73,19 @@
         pl.semaphore_signal(barrier, inc=1, device_id=at_z(k), device_id_type=MESH)
     for k in range(1, NX):
         pl.semaphore_signal(barrier, inc=1, device_id=at_x(k), device_id_type=MESH)
-    for k in range(1, NDP):
-        pl.semaphore_signal(barrier, inc=1, device_id=at_d(k), device_id_type=MESH)
-
-    for c in range(NC):
+    for k in range(1, NY):
+        pl.semaphore_signal(barrier, inc=1, device_id=at_y(k), device_id_type=MESH)
+    pl.semaphore_signal(barrier, inc=1, device_id=other_core, device_id_type=MESH)
+
+    def own_block(c):
         for d in range(NDP):
             ring[c, 0, :, d * cols:(d + 1) * cols] = cot_ref[
                 :, d * own_cols + c * cols:d * own_cols + (c + 1) * cols
             ]
-    for c in range(2):
-        for d in range(NDP):
-            w_load(c, d).start()
-    pl.semaphore_wait(barrier, NZ - 1 + NX - 1 + NDP - 1)
+
+    own_block(0)
+    own_block(1)
+    pl.semaphore_wait(barrier, NZ - 1 + NX - 1 + NY)
 
     def ring_copy(c, s, right):
         off = -s if right else s
@@ -95,8 +101,14 @@
             at_z(1 if right else -1),
         )
 
-    ring_copy(0, 0, True).start()
-    ring_copy(0, 0, False).start()
+    for c in range(2):
+        ring_copy(c, 0, True).start()
+        ring_copy(c, 0, False).start()
+    for c in range(2):
+        for d in range(NDP):
+            w_load(c, d).start()
+    for c in range(2, NC):
+        own_block(c)
 
     mod = jnp.broadcast_to(mod_ref[...], (8, tok))
     kinds = [(mod == m).astype(F32) for m in range(3)]
@@ -179,23 +191,23 @@
         pick = jnp.where(wanted == dests[slot, 0:1, :], 1.0, 0.0).astype(BF16)
         got = jnp.dot(pick, ring[c, slot], preferred_element_type=F32).astype(BF16)
         for x in range(NX):
-            staged[c % 2, x, slot] = got[x * CAP:(x + 1) * CAP]
+            staged[c, x, slot] = got[x * CAP:(x + 1) * CAP]
         lands = cot_got.at[c, my_x, (my_z + off + NZ) % NZ]
         for k in range(NX):
-            src = staged.at[c % 2, (my_x + k) % NX, slot]
+            src = staged.at[c, (my_x + k) % NX, slot]
             if k == 0:
                 pltpu.make_async_copy(src, lands, x_own.at[c]).start()
             else:
                 remote(src, lands, x_send.at[c, k], x_recv.at[c, NX - k], at_x(k)).start()
 
     def chunk_arrived(c):
-        wait_bytes(staged.at[c % 2, 0], x_own.at[c])
+        wait_bytes(staged.at[c, 0], x_own.at[c])
         for k in range(1, NX):
-            wait_bytes(staged.at[c % 2, k], x_recv.at[c, k])
+            wait_bytes(staged.at[c, k], x_recv.at[c, k])
 
     def x_sends_done(c):
         for k in range(1, NX):
-            wait_bytes(staged.at[c % 2, k], x_send.at[c, k])
+            wait_bytes(staged.at[c, k], x_send.at[c, k])
 
     def input_grad(c):
         wait_bytes(w_chunk.at[c % 2], w_sem.at[c])
@@ -218,22 +230,31 @@
             for d in range(NDP):
                 w_load(c + 2, d).start()
 
+    def pair_copy(c):
+        return remote(
+            partial.at[c % 2, 1 - my_core], other.at[c], pair_send.at[c], pair_recv.at[c], other_core
+        )
+
     def rs_copy(c, k):
         return remote(
-            partial.at[c % 2, (my_d + k) % NDP], terms.at[c, my_d],
-            rs_send.at[c, k], rs_recv.at[c, NDP - k], at_d(k),
+            partial.at[c % 2, my_core, (my_y + k) % NY], terms.at[c, my_y],
+            rs_send.at[c, k], rs_recv.at[c, NY - k], at_y(k),
         )
 
     def rs_own_copy(c):
-        return pltpu.make_async_copy(partial.at[c % 2, my_d], terms.at[c, my_d], rs_own.at[c])
+        return pltpu.make_async_copy(
+            partial.at[c % 2, my_core, my_y], terms.at[c, my_y], rs_own.at[c]
+        )
+
+    def weight_sends_done(c):
+        pair_copy(c).wait_send()
+        for k in range(1, NY):
+            rs_copy(c, k).wait_send()
+        rs_own_copy(c).wait()
 
     def weight_grad(c):
         if c >= 2:
-            for k in range(1, NDP):
-                rs_copy(c - 2, k).wait_send()
-            rs_own_copy(c - 2).wait()
-
-        per_tile = TILE // cols
+            weight_sends_done(c - 2)
 
         @pl.loop(0, width // TILE)
         def _(j):
@@ -242,25 +263,37 @@
                 attn_t[...], cot_got[c, :, :, :, at].reshape(NX * NZ * CAP, TILE),
                 preferred_element_type=F32,
             ).astype(BF16)
-            for i in range(per_tile):
-                partial[c % 2, j * per_tile + i] = term[:, i * cols:(i + 1) * cols]
+            for i in range(CORES):
+                partial[c % 2, i, j] = term[:, i * cols:(i + 1) * cols]
+
+        pair_copy(c).start()
+
+    def weight_pair(c):
+        pair_copy(c).wait_recv()
+
+        @pl.loop(0, feats // TILE)
+        def _(j):
+            at = pl.ds(pl.multiple_of(j * TILE, TILE), TILE)
+            for y in range(NY):
+                both = partial[c % 2, my_core, y, at, :].astype(F32) + other[c, y, at, :].astype(F32)
+                partial[c % 2, my_core, y, at, :] = both.astype(BF16)
 
         rs_own_copy(c).start()
-        for k in range(1, NDP):
+        for k in range(1, NY):
             rs_copy(c, k).start()
 
     def weight_grad_sum(c):
         if c >= NC - 2:
             rs_own_copy(c).wait()
-        for k in range(1, NDP):
+        for k in range(1, NY):
             rs_copy(c, k).wait_recv()
 
         @pl.loop(0, feats // TILE)
         def _(j):
             at = pl.ds(pl.multiple_of(j * TILE, TILE), TILE)
             total = terms[c, 0, at, :].astype(F32)
-            for d in range(1, NDP):
-                total += terms[c, d, at, :].astype(F32)
+            for y in range(1, NY):
+                total += terms[c, y, at, :].astype(F32)
             wgrad_ref[at, c * cols:(c + 1) * cols] = total.astype(BF16)
 
     def ret_z_copy(k):
@@ -268,47 +301,55 @@
             grads.at[:, (my_z + k) % NZ], ret_z.at[my_z], rz_send.at[k], rz_recv.at[NZ - k], at_z(k)
         )
 
-    for tick in range(2 * NC + LAST):
-        live = [(c, tick - 2 * c) for c in range(NC) if 0 <= tick - 2 * c < 8]
-        for c, s in live:
-            if s in range(1, LAST + 1):
-                ring_copy(c, s - 1, True).wait_recv()
-                ring_copy(c, s - 1, False).wait_recv()
-            if s < LAST and (c, s) != (0, 0):
-                ring_copy(c, s, True).start()
-                ring_copy(c, s, False).start()
-        if tick == 1:
+    def ring_step(c, s):
+        if s > 0:
+            ring_copy(c, s - 1, True).wait_recv()
+            ring_copy(c, s - 1, False).wait_recv()
+        if s < LAST and (c >= 2 or s > 0):
+            ring_copy(c, s, True).start()
+            ring_copy(c, s, False).start()
+        if (c, s) == (0, 1):
             for k in range(1, NZ):
                 dest_copy(k).wait_recv()
-        if tick == 2:
-            attn_along_z()
-        for c, s in live:
-            if s == 0:
-                if c < 2:
-                    deliver(c, 0)
-            elif s < LAST:
-                if s == 1 and c >= 2:
-                    x_sends_done(c - 2)
-                    deliver(c, 0)
-                deliver(c, -s)
-                deliver(c, s)
-            elif s == LAST:
-                deliver(c, LAST)
-            elif s == LAST + 1:
-                chunk_arrived(c)
-                if c == 0:
-                    attn_arrived()
-                input_grad(c)
-                if c == NC - 1:
-                    pltpu.make_async_copy(grads.at[:, my_z], ret_z.at[my_z], rz_own).start()
-                    for k in range(1, NZ):
-                        ret_z_copy(k).start()
-                weight_grad(c)
-                if c == 2:
-                    weight_grad_sum(0)
-
-    for c in range(1, NC - 1):
-        weight_grad_sum(c)
+        if s in (0, LAST):
+            deliver(c, s)
+        else:
+            deliver(c, -s)
+            deliver(c, s)
+
+    for c, s in ((0, 0), (1, 0), (0, 1), (1, 1), (0, 2)):
+        ring_step(c, s)
+    attn_along_z()
+    for c, s in ((1, 2), (0, 3), (2, 0), (1, 3), (3, 0), (0, 4), (2, 1), (1, 4), (3, 1)):
+        ring_step(c, s)
+    chunk_arrived(0)
+    input_grad(0)
+    ring_step(2, 2)
+    attn_arrived()
+    weight_grad(0)
+    ring_step(3, 2)
+    chunk_arrived(1)
+    input_grad(1)
+    ring_step(2, 3)
+    weight_grad(1)
+    weight_pair(0)
+    ring_step(3, 3)
+    weight_pair(1)
+    ring_step(2, 4)
+    ring_step(3, 4)
+    chunk_arrived(2)
+    input_grad(2)
+    chunk_arrived(3)
+    input_grad(3)
+    pltpu.make_async_copy(grads.at[:, my_z], ret_z.at[my_z], rz_own).start()
+    for k in range(1, NZ):
+        ret_z_copy(k).start()
+    weight_grad(2)
+    weight_grad(3)
+    weight_pair(2)
+    weight_pair(3)
+    weight_grad_sum(0)
+    weight_grad_sum(1)
 
     def ret_x_start(z):
         for k in range(NX):
@@ -323,7 +364,8 @@
     for k in (1, 7, 2, 6, 3, 5, 4):
         ret_z_copy(k).wait_recv()
         ret_x_start((my_z - k + NZ) % NZ)
-    weight_grad_sum(NC - 1)
+    weight_grad_sum(2)
+    weight_grad_sum(3)
     for k in range(NX):
         wait_bytes(ret_x.at[k], rx_own if k == 0 else rx_recv.at[k])
 
@@ -347,9 +389,10 @@
         for s in range(LAST):
             ring_copy(c, s, True).wait_send()
             ring_copy(c, s, False).wait_send()
+        x_sends_done(c)
     for c in range(NC - 2, NC):
-        x_sends_done(c)
-        for k in range(1, NDP):
+        pair_copy(c).wait_send()
+        for k in range(1, NY):
             rs_copy(c, k).wait_send()
 
 
@@ -373,11 +416,12 @@
         scratch_shapes=[
             pltpu.VMEM((NC, NZ, tok, width), BF16),
             pltpu.VMEM((NZ, 8, tok), jnp.int32),
-            pltpu.VMEM((2, NX, NZ, CAP, width), BF16),
+            pltpu.VMEM((NC, NX, NZ, CAP, width), BF16),
             pltpu.VMEM((NC, NX, NZ, CAP, width), BF16),
             pltpu.VMEM((2, feats, width), BF16),
-            pltpu.VMEM((2, NDP, feats, width // NDP), BF16),
-            pltpu.VMEM((NC, NDP, feats, width // NDP), BF16),
+            pltpu.VMEM((2, CORES, NY, feats, width // NDP), BF16),
+            pltpu.VMEM((NC, NY, feats, width // NDP), BF16),
+            pltpu.VMEM((NC, NY, feats, width // NDP), BF16),
             pltpu.VMEM((NX * NZ * CAP, feats), F32),
             pltpu.VMEM((NX, HALVES, CAP, model), BF16),
             pltpu.VMEM((NX, HALVES, CAP, model), BF16),
@@ -392,7 +436,7 @@
             dma((NX,)), dma((NX,)), dma,
             dma((NZ,)), dma((NZ,)), dma,
             dma((NC,)),
-            dma((NC, NDP)), dma((NC, NDP)), dma((NC,)),
+            dma((NC,)), dma((NC,)), dma((NC, NY)), dma((NC, NY)), dma((NC,)),
             dma((NZ,)), dma((NZ,)), dma,
             dma((NX,)), dma((NX,)), dma,
         ],

time: 198 us -> 190 us (0.960)
  Pallas kernels: 192 us -> 185 us
    pallas_call x1, Pallas kernels: 192 us -> 185 us  [backward(): pl.pallas_call(kernel, out_shape=(jax.ShapeDtypeStruct((tok, model), BF16...]
where the time goes in v4:
time: 190 us
  Pallas kernels  185 us (97%)
  local copies, waits for them, and re-layouts  4.55 us (2%)
    pallas_call x1, Pallas kernels, backward(): pl.pallas_call(kernel, out_shape=(jax.ShapeDtypeStruct((tok, model), BF16...  185 us
    unnamed x2, local copies, waits for them, and re-layouts  4.55 us

profile of v4, /device:TPU:8, one launch (start us, length us, event | category | flops | bytes accessed | tf_op | source)
XLA Modules:
  0.0 189.7 jit_solution(13264042501897752068)
XLA Ops:
  0.6 184.5 %moe_proj_backward.1 = (bf16[128,4096]{1,0:T(8,128)(2,1)}, bf16[1024,512]{1,0:T(8,128)(2,1)}) custom-call(s32[1,128]{1,0:T(1,128)} %bitcast.1, s32[8]{0:T(128)} %gm_ref.1, bf16[128,4096]{1,0:T(8,128)(2,1)} %attn_ref.1, bf16[128,4096]{1,0:T(8,128)(2,1)} %cot_ref.1, bf16[1024,4096]{1,0:T(8,128)(2,1)} %w_ref.1), custom_call_target="tpu_custom_call" | custom-call | tf_op jit(solution)/shard_map/moe_proj_backward/pallas_call | solution.py:405
  185.2 2.3 %copy.9 = bf16[128,4096]{1,0:T(8,128)(2,1)} copy(bf16[128,4096]{1,0:T(8,128)(2,1)} %get-tuple-element.4) | data formatting | bytes 2097152
  187.5 2.3 %copy.10 = bf16[1024,512]{1,0:T(8,128)(2,1)} copy(bf16[1024,512]{1,0:T(8,128)(2,1)} %get-tuple-element.5) | data formatting | bytes 2097152

commit v5 on v4

--- a/solution.py
+++ b/solution.py
@@ -14,6 +14,7 @@
 NDP = 8
 CORES = 2
 NY = NDP // CORES
+SOURCES = ((0, -1, 1), (-2, 2), (-3, 3), (4,))
 NC = 4
 LAST = NZ // 2
 TILE = 256
@@ -23,15 +24,15 @@
 
 
 def kernel(
-    mod_ref, gm_ref, attn_ref, cot_ref, w_ref, grad_ref, wgrad_ref,
-    ring, dests, staged, cot_got, w_chunk, partial, other, terms, acc,
+    mod_ref, gm_ref, attn_hbm, cot_hbm, w_ref, grad_ref, wgrad_ref,
+    attn_ref, ring, dests, staged, cot_got, w_chunk, partial, other, terms, acc,
     attn_own, attn_x, attn_got, attn_t, grads, ret_z, ret_x,
-    dest_send, dest_recv, right_send, right_recv, left_send, left_recv,
+    attn_in, cot_in, dest_send, dest_recv, right_send, right_recv, left_send, left_recv,
     x_send, x_recv, x_own, ax_send, ax_recv, ax_own, az_send, az_recv, az_own,
     w_sem, pair_send, pair_recv, rs_send, rs_recv, rs_own, rz_send, rz_recv, rz_own, rx_send, rx_recv, rx_own,
 ):
-    tok = cot_ref.shape[0]
-    width = cot_ref.shape[1] // NC
+    tok = cot_hbm.shape[0]
+    width = cot_hbm.shape[1] // NC
     cols = width // NDP
     own_cols = wgrad_ref.shape[1]
     feats = w_ref.shape[0]
@@ -68,6 +69,15 @@
             w_sem.at[c],
         )
 
+    def own_block(c):
+        for d in range(NDP):
+            pltpu.make_async_copy(
+                cot_hbm.at[:, pl.ds(d * own_cols + c * cols, cols)],
+                ring.at[c, 0, :, pl.ds(d * cols, cols)],
+                cot_in.at[c],
+            ).start()
+
+    attn_load = pltpu.make_async_copy(attn_hbm, attn_ref, attn_in)
     barrier = pltpu.get_barrier_semaphore()
     for k in range(1, NZ):
         pl.semaphore_signal(barrier, inc=1, device_id=at_z(k), device_id_type=MESH)
@@ -77,14 +87,9 @@
         pl.semaphore_signal(barrier, inc=1, device_id=at_y(k), device_id_type=MESH)
     pl.semaphore_signal(barrier, inc=1, device_id=other_core, device_id_type=MESH)
 
-    def own_block(c):
-        for d in range(NDP):
-            ring[c, 0, :, d * cols:(d + 1) * cols] = cot_ref[
-                :, d * own_cols + c * cols:d * own_cols + (c + 1) * cols
-            ]
-
     own_block(0)
     own_block(1)
+    attn_load.start()
     pl.semaphore_wait(barrier, NZ - 1 + NX - 1 + NY)
 
     def ring_copy(c, s, right):
@@ -102,13 +107,14 @@
         )
 
     for c in range(2):
+        wait_bytes(ring.at[c, 0], cot_in.at[c])
         ring_copy(c, 0, True).start()
         ring_copy(c, 0, False).start()
+    for c in range(2, NC):
+        own_block(c)
     for c in range(2):
         for d in range(NDP):
             w_load(c, d).start()
-    for c in range(2, NC):
-        own_block(c)
 
     mod = jnp.broadcast_to(mod_ref[...], (8, tok))
     kinds = [(mod == m).astype(F32) for m in range(3)]
@@ -139,6 +145,7 @@
         dest_copy(k).start()
 
     slots = lax.broadcasted_iota(jnp.int32, (NGROUP * CAP, tok), 0)
+    attn_load.wait()
     pick_own = jnp.where(slots == dest[0:1], 1.0, 0.0).astype(BF16)
     for p in range(PIECES):
         got = jnp.dot(pick_own, attn_ref[:, p * feats:(p + 1) * feats], preferred_element_type=F32)
@@ -192,18 +199,23 @@
         got = jnp.dot(pick, ring[c, slot], preferred_element_type=F32).astype(BF16)
         for x in range(NX):
             staged[c, x, slot] = got[x * CAP:(x + 1) * CAP]
+        part = abs(off) - 1 if off else 0
         lands = cot_got.at[c, my_x, (my_z + off + NZ) % NZ]
         for k in range(NX):
             src = staged.at[c, (my_x + k) % NX, slot]
             if k == 0:
-                pltpu.make_async_copy(src, lands, x_own.at[c]).start()
+                pltpu.make_async_copy(src, lands, x_own.at[c, part]).start()
             else:
-                remote(src, lands, x_send.at[c, k], x_recv.at[c, NX - k], at_x(k)).start()
-
-    def chunk_arrived(c):
-        wait_bytes(staged.at[c, 0], x_own.at[c])
-        for k in range(1, NX):
-            wait_bytes(staged.at[c, k], x_recv.at[c, k])
+                remote(
+                    src, lands, x_send.at[c, k], x_recv.at[c, part, NX - k], at_x(k)
+                ).start()
+
+    def arrived(c, parts):
+        for part in parts:
+            count = len(SOURCES[part])
+            wait_bytes(staged.at[c, 0, pl.ds(0, count)], x_own.at[c, part])
+            for k in range(1, NX):
+                wait_bytes(staged.at[c, k, pl.ds(0, count)], x_recv.at[c, part, k])
 
     def x_sends_done(c):
         for k in range(1, NX):
@@ -219,16 +231,35 @@
                 cot_got[c].reshape(NX * NZ * CAP, width), w_chunk[c % 2, at, :],
                 (((1,), (1,)), ((), ())), preferred_element_type=F32,
             )
-            if c > 0:
-                term += acc[:, at]
-            if c < NC - 1:
-                acc[:, at] = term
+            term = term.reshape(NX, NZ, CAP, TILE)
+            acc[:, :, :, at] = term if c == 0 else acc[:, :, :, at] + term
+
+        for d in range(NDP):
+            w_load(c + 2, d).start()
+
+    def rows_grad(offsets):
+        zs = [(my_z + off + NZ) % NZ for off in offsets]
+        count = NX * CAP
+
+        @pl.loop(0, feats // TILE)
+        def _(j):
+            at = pl.ds(pl.multiple_of(j * TILE, TILE), TILE)
+            term = sum(
+                lax.dot_general(
+                    jnp.concatenate([cot_got[c, :, z].reshape(count, width) for z in zs], 0),
+                    w_chunk[c % 2, at, :], (((1,), (1,)), ((), ())), preferred_element_type=F32,
+                )
+                for c in range(NC - 2, NC)
+            )
+            for i, z in enumerate(zs):
+                total = term[i * count:(i + 1) * count].reshape(NX, CAP, TILE) + acc[:, z, :, at]
+                grads[:, z, :, at] = total.astype(BF16)
+
+        for off in offsets:
+            if off == 0:
+                pltpu.make_async_copy(grads.at[:, my_z], ret_z.at[my_z], rz_own).start()
             else:
-                grads[:, :, :, at] = term.astype(BF16).reshape(NX, NZ, CAP, TILE)
-
-        if c + 2 < NC:
-            for d in range(NDP):
-                w_load(c + 2, d).start()
+                ret_z_copy(off % NZ).start()
 
     def pair_copy(c):
         return remote(
@@ -302,6 +333,8 @@
         )
 
     def ring_step(c, s):
+        if c >= 2 and s == 0:
+            wait_bytes(ring.at[c, 0], cot_in.at[c])
         if s > 0:
             ring_copy(c, s - 1, True).wait_recv()
             ring_copy(c, s - 1, False).wait_recv()
@@ -322,33 +355,37 @@
     attn_along_z()
     for c, s in ((1, 2), (0, 3), (2, 0), (1, 3), (3, 0), (0, 4), (2, 1), (1, 4), (3, 1)):
         ring_step(c, s)
-    chunk_arrived(0)
+    every = range(len(SOURCES))
+    arrived(0, every)
     input_grad(0)
     ring_step(2, 2)
     attn_arrived()
     weight_grad(0)
     ring_step(3, 2)
-    chunk_arrived(1)
+    arrived(1, every)
     input_grad(1)
     ring_step(2, 3)
+    for c in range(NC - 2, NC):
+        wait_bytes(w_chunk.at[c % 2], w_sem.at[c])
+        arrived(c, (0,))
+    rows_grad(SOURCES[0])
+    ring_step(3, 3)
     weight_grad(1)
     weight_pair(0)
-    ring_step(3, 3)
+    ring_step(2, 4)
+    for c in range(NC - 2, NC):
+        arrived(c, (1,))
+    rows_grad(SOURCES[1])
     weight_pair(1)
-    ring_step(2, 4)
     ring_step(3, 4)
-    chunk_arrived(2)
-    input_grad(2)
-    chunk_arrived(3)
-    input_grad(3)
-    pltpu.make_async_copy(grads.at[:, my_z], ret_z.at[my_z], rz_own).start()
-    for k in range(1, NZ):
-        ret_z_copy(k).start()
+    arrived(2, (2, 3))
     weight_grad(2)
+    arrived(3, (2, 3))
+    rows_grad(SOURCES[2] + SOURCES[3])
+    weight_pair(2)
     weight_grad(3)
-    weight_pair(2)
+    weight_grad_sum(0)
     weight_pair(3)
-    weight_grad_sum(0)
     weight_grad_sum(1)
 
     def ret_x_start(z):
@@ -402,6 +439,7 @@
     feats = w.shape[0]
     dma = pltpu.SemaphoreType.DMA
     vmem = pl.BlockSpec(memory_space=pltpu.VMEM)
+    hbm = pl.BlockSpec(memory_space=pl.ANY)
     return pl.pallas_call(
         kernel,
         out_shape=(
@@ -409,11 +447,11 @@
             jax.ShapeDtypeStruct((feats, model // NDP), BF16),
         ),
         in_specs=[
-            vmem, pl.BlockSpec(memory_space=pltpu.SMEM), vmem, vmem,
-            pl.BlockSpec(memory_space=pl.ANY),
+            vmem, pl.BlockSpec(memory_space=pltpu.SMEM), hbm, hbm, hbm,
         ],
         out_specs=(vmem, vmem),
         scratch_shapes=[
+            pltpu.VMEM((tok, model), BF16),
             pltpu.VMEM((NC, NZ, tok, width), BF16),
             pltpu.VMEM((NZ, 8, tok), jnp.int32),
             pltpu.VMEM((NC, NX, NZ, CAP, width), BF16),
@@ -422,7 +460,7 @@
             pltpu.VMEM((2, CORES, NY, feats, width // NDP), BF16),
             pltpu.VMEM((NC, NY, feats, width // NDP), BF16),
             pltpu.VMEM((NC, NY, feats, width // NDP), BF16),
-            pltpu.VMEM((NX * NZ * CAP, feats), F32),
+            pltpu.VMEM((NX, NZ, CAP, feats), F32),
             pltpu.VMEM((NX, HALVES, CAP, model), BF16),
             pltpu.VMEM((NX, HALVES, CAP, model), BF16),
             pltpu.VMEM((NX, NZ, CAP, feats), BF16),
@@ -430,9 +468,9 @@
             pltpu.VMEM((NX, NZ, CAP, feats), BF16),
             pltpu.VMEM((NZ, NX, CAP, feats), BF16),
             pltpu.VMEM((NX, NZ, CAP, feats), BF16),
-            dma((NZ,)), dma((NZ,)),
+            dma, dma((NC,)), dma((NZ,)), dma((NZ,)),
             dma((NC, LAST)), dma((NC, LAST)), dma((NC, LAST)), dma((NC, LAST)),
-            dma((NC, NX)), dma((NC, NX)), dma((NC,)),
+            dma((NC, NX)), dma((NC, LAST, NX)), dma((NC, LAST)),
             dma((NX,)), dma((NX,)), dma,
             dma((NZ,)), dma((NZ,)), dma,
             dma((NC,)),

time: 190 us -> 182 us (0.958); the launches traced: 190 us -> 178 us
  Pallas kernels: 185 us -> 173 us
    pallas_call x1, Pallas kernels: 185 us -> 173 us  [backward(): pl.pallas_call(kernel, out_shape=(jax.ShapeDtypeStruct((tok, model), BF16...]
where the time goes in v5:
time: 182 us; the launch traced here: 178 us
  Pallas kernels  173 us (95%)
  local copies, waits for them, and re-layouts  4.55 us (2%)
    pallas_call x1, Pallas kernels, backward(): pl.pallas_call(kernel, out_shape=(jax.ShapeDtypeStruct((tok, model), BF16...  173 us
    unnamed x2, local copies, waits for them, and re-layouts  4.55 us

profile of v5, /device:TPU:8, one launch (start us, length us, event | category | flops | bytes accessed | tf_op | source)
XLA Modules:
  0.0 178.2 jit_solution(11132994690051894185)
XLA Ops:
  0.6 173.1 %moe_proj_backward.1 = (bf16[128,4096]{1,0:T(8,128)(2,1)}, bf16[1024,512]{1,0:T(8,128)(2,1)}) custom-call(s32[1,128]{1,0:T(1,128)} %bitcast.1, s32[8]{0:T(128)} %gm_ref.1, bf16[128,4096]{1,0:T(8,128)(2,1)} %attn_hbm.1, bf16[128,4096]{1,0:T(8,128)(2,1)} %cot_hbm.1, bf16[1024,4096]{1,0:T(8,128)(2,1)} %w_ref.1), custom_call_target="tpu_custom_call" | custom-call | tf_op jit(solution)/shard_map/moe_proj_backward/pallas_call | solution.py:443
  173.7 2.3 %copy.9 = bf16[128,4096]{1,0:T(8,128)(2,1)} copy(bf16[128,4096]{1,0:T(8,128)(2,1)} %get-tuple-element.4) | data formatting | bytes 2097152
  176.0 2.3 %copy.10 = bf16[1024,512]{1,0:T(8,128)(2,1)} copy(bf16[1024,512]{1,0:T(8,128)(2,1)} %get-tuple-element.5) | data formatting | bytes 2097152

commit v6 on v5

--- a/solution.py
+++ b/solution.py
@@ -353,39 +353,43 @@
     for c, s in ((0, 0), (1, 0), (0, 1), (1, 1), (0, 2)):
         ring_step(c, s)
     attn_along_z()
-    for c, s in ((1, 2), (0, 3), (2, 0), (1, 3), (3, 0), (0, 4), (2, 1), (1, 4), (3, 1)):
+    every = range(len(SOURCES))
+    for c, s in ((1, 2), (0, 3), (2, 0), (1, 3), (3, 0), (0, 4), (2, 1), (1, 4)):
         ring_step(c, s)
-    every = range(len(SOURCES))
     arrived(0, every)
     input_grad(0)
+    ring_step(3, 1)
+    arrived(1, every)
+    input_grad(1)
     ring_step(2, 2)
     attn_arrived()
     weight_grad(0)
     ring_step(3, 2)
-    arrived(1, every)
-    input_grad(1)
+    weight_grad(1)
+    weight_pair(0)
     ring_step(2, 3)
     for c in range(NC - 2, NC):
         wait_bytes(w_chunk.at[c % 2], w_sem.at[c])
         arrived(c, (0,))
     rows_grad(SOURCES[0])
     ring_step(3, 3)
-    weight_grad(1)
-    weight_pair(0)
-    ring_step(2, 4)
+    weight_pair(1)
     for c in range(NC - 2, NC):
         arrived(c, (1,))
     rows_grad(SOURCES[1])
-    weight_pair(1)
+    ring_step(2, 4)
+    for c in range(NC - 2, NC):
+        arrived(c, (2,))
+    rows_grad(SOURCES[2])
     ring_step(3, 4)
-    arrived(2, (2, 3))
+    arrived(2, (3,))
     weight_grad(2)
-    arrived(3, (2, 3))
-    rows_grad(SOURCES[2] + SOURCES[3])
+    arrived(3, (3,))
+    rows_grad(SOURCES[3])
     weight_pair(2)
     weight_grad(3)
+    weight_pair(3)
     weight_grad_sum(0)
-    weight_pair(3)
     weight_grad_sum(1)
 
     def ret_x_start(z):
@@ -485,8 +489,38 @@
     )(mod, gm, attn, cot, w)
 
 
+def hand_over(values):
+    parts = 8
+
+    def body(*refs):
+        copies = []
+        for i, value in enumerate(values):
+            rows = value.shape[0] // parts
+            for k in range(parts):
+                at = pl.ds(k * rows, rows)
+                copies.append(pltpu.make_async_copy(
+                    refs[i].at[at], refs[len(values) + i].at[at], refs[-1].at[i, k]
+                ))
+        for copy in copies:
+            copy.start()
+        for copy in copies:
+            copy.wait()
+
+    hbm = pl.BlockSpec(memory_space=pl.ANY)
+    return pl.pallas_call(
+        body,
+        out_shape=tuple(jax.ShapeDtypeStruct(v.shape, v.dtype) for v in values),
+        in_specs=[hbm] * len(values),
+        out_specs=(hbm,) * len(values),
+        scratch_shapes=[pltpu.SemaphoreType.DMA((len(values), parts))],
+        name="hand_over",
+    )(*values)
+
+
 def per_device(attn_out, out_cot, modality, group_modality, o_weight):
-    return backward(modality.reshape(1, -1), group_modality, attn_out, out_cot, o_weight)
+    return hand_over(
+        backward(modality.reshape(1, -1), group_modality, attn_out, out_cot, o_weight)
+    )
 
 
 def solution(mesh):

time: 182 us -> 233 us (1.28)
  Pallas kernels: 173 us -> 231 us
  local copies, waits for them, and re-layouts: 4.55 us -> 0 us
    pallas_call x0 -> x1, Pallas kernels: none -> 64.8 us  [hand_over(): pl.pallas_call(body, out_shape=tuple((jax.ShapeDtypeStruct(v.shape, v.dty...]
    pallas_call x1, Pallas kernels: 173 us -> 166 us  [backward(): pl.pallas_call(kernel, out_shape=(jax.ShapeDtypeStruct((tok, model), BF16...]
    unnamed x2 -> x0, local copies, waits for them, and re-layouts: 4.55 us -> none
where the time goes in v6:
time: 233 us; the launch traced here: 231 us
  Pallas kernels  231 us (99%)
    pallas_call x1, Pallas kernels, backward(): pl.pallas_call(kernel, out_shape=(jax.ShapeDtypeStruct((tok, model), BF16...  166 us
    pallas_call x1, Pallas kernels, hand_over(): pl.pallas_call(body, out_shape=tuple((jax.ShapeDtypeStruct(v.shape, v.dty...  64.8 us

profile of v6, /device:TPU:8, one launch (start us, length us, event | category | flops | bytes accessed | tf_op | source)
XLA Modules:
  0.0 231.3 jit_solution(13657837083207856923)
XLA Ops:
  0.6 165.8 %moe_proj_backward.1 = (bf16[128,4096]{1,0:T(8,128)(2,1)}, bf16[1024,512]{1,0:T(8,128)(2,1)}) custom-call(s32[1,128]{1,0:T(1,128)} %bitcast.1, s32[8]{0:T(128)} %gm_ref.1, bf16[128,4096]{1,0:T(8,128)(2,1)} %attn_hbm.1, bf16[128,4096]{1,0:T(8,128)(2,1)} %cot_hbm.1, bf16[1024,4096]{1,0:T(8,128)(2,1)} %w_ref.1), custom_call_target="tpu_custom_call" | custom-call | tf_op jit(solution)/shard_map/moe_proj_backward/pallas_call | solution.py:447
  166.5 64.8 %hand_over.1 = (bf16[128,4096]{1,0:T(8,128)(2,1)}, bf16[1024,512]{1,0:T(8,128)(2,1)}) custom-call(bf16[128,4096]{1,0:T(8,128)(2,1)} %get-tuple-element.4.refs_0_, bf16[1024,512]{1,0:T(8,128)(2,1)} %get-tuple-element.5.refs_1_), custom_call_target="tpu_custom_call" | custom-call | tf_op jit(solution)/shard_map/hand_over/pallas_call | solution.py:510

commit v7 on v6

--- a/solution.py
+++ b/solution.py
@@ -24,9 +24,9 @@
 
 
 def kernel(
-    mod_ref, gm_ref, attn_hbm, cot_hbm, w_ref, grad_ref, wgrad_ref,
+    mod_ref, gm_ref, attn_hbm, cot_hbm, w_ref, ret_x, dest_ref, wgrad_ref,
     attn_ref, ring, dests, staged, cot_got, w_chunk, partial, other, terms, acc,
-    attn_own, attn_x, attn_got, attn_t, grads, ret_z, ret_x,
+    attn_own, attn_x, attn_got, attn_t, grads, ret_z,
     attn_in, cot_in, dest_send, dest_recv, right_send, right_recv, left_send, left_recv,
     x_send, x_recv, x_own, ax_send, ax_recv, ax_own, az_send, az_recv, az_own,
     w_sem, pair_send, pair_recv, rs_send, rs_recv, rs_own, rz_send, rz_recv, rz_own, rx_send, rx_recv, rx_own,
@@ -137,6 +137,7 @@
         routed = jnp.where((mod == serves[g]) & (target == rank), g, routed)
     dest = routed * CAP + jnp.floor((order + 0.5) / per).astype(jnp.int32)
     dests[0] = dest
+    dest_ref[...] = dest
 
     def dest_copy(k):
         return remote(dests.at[0], dests.at[NZ - k], dest_send.at[k], dest_recv.at[NZ - k], at_z(k))
@@ -410,15 +411,6 @@
     for k in range(NX):
         wait_bytes(ret_x.at[k], rx_own if k == 0 else rx_recv.at[k])
 
-    back = jnp.where(slots == dests[0, 0:1, :], 1.0, 0.0).astype(BF16)
-    for p in range(PIECES):
-        pieces = jnp.concatenate(
-            [ret_x[g // HALVES, (g % HALVES) * PIECES + p] for g in range(NGROUP)], 0
-        )
-        grad_ref[:, p * feats:(p + 1) * feats] = lax.dot_general(
-            back, pieces, (((0,), (0,)), ((), ())), preferred_element_type=F32
-        ).astype(BF16)
-
     for k in range(1, NZ):
         dest_copy(k).wait_send()
         attn_z_copy(k).wait_send()
@@ -447,13 +439,14 @@
     return pl.pallas_call(
         kernel,
         out_shape=(
-            jax.ShapeDtypeStruct((tok, model), BF16),
+            jax.ShapeDtypeStruct((NX, NZ, CAP, feats), BF16),
+            jax.ShapeDtypeStruct((8, tok), jnp.int32),
             jax.ShapeDtypeStruct((feats, model // NDP), BF16),
         ),
         in_specs=[
             vmem, pl.BlockSpec(memory_space=pltpu.SMEM), hbm, hbm, hbm,
         ],
-        out_specs=(vmem, vmem),
+        out_specs=(hbm, vmem, vmem),
         scratch_shapes=[
             pltpu.VMEM((tok, model), BF16),
             pltpu.VMEM((NC, NZ, tok, width), BF16),
@@ -471,7 +464,6 @@
             pltpu.VMEM((feats, NX * NZ * CAP), BF16),
             pltpu.VMEM((NX, NZ, CAP, feats), BF16),
             pltpu.VMEM((NZ, NX, CAP, feats), BF16),
-            pltpu.VMEM((NX, NZ, CAP, feats), BF16),
             dma, dma((NC,)), dma((NZ,)), dma((NZ,)),
             dma((NC, LAST)), dma((NC, LAST)), dma((NC, LAST)), dma((NC, LAST)),
             dma((NC, NX)), dma((NC, LAST, NX)), dma((NC, LAST)),
@@ -489,38 +481,81 @@
     )(mod, gm, attn, cot, w)
 
 
-def hand_over(values):
-    parts = 8
-
-    def body(*refs):
-        copies = []
-        for i, value in enumerate(values):
-            rows = value.shape[0] // parts
-            for k in range(parts):
-                at = pl.ds(k * rows, rows)
-                copies.append(pltpu.make_async_copy(
-                    refs[i].at[at], refs[len(values) + i].at[at], refs[-1].at[i, k]
-                ))
-        for copy in copies:
-            copy.start()
-        for copy in copies:
-            copy.wait()
-
+def finish_kernel(
+    dest_ref, ret_hbm, w_hbm, grad_hbm, w_out, ret, grad, wgrad, ret_in, grad_out, w_in, w_sent,
+):
+    tok, feats = dest_ref.shape[1], ret.shape[3]
+    parts = w_in.shape[0]
+    rows = wgrad.shape[0] // parts
+
+    def ret_load(p, h):
+        at = h * PIECES + p
+        return pltpu.make_async_copy(ret_hbm.at[:, at], ret.at[:, at], ret_in.at[at])
+
+    def w_load(k):
+        at = pl.ds(k * rows, rows)
+        return pltpu.make_async_copy(w_hbm.at[at], wgrad.at[at], w_in.at[k])
+
+    def w_store(k):
+        at = pl.ds(k * rows, rows)
+        return pltpu.make_async_copy(wgrad.at[at], w_out.at[at], w_sent.at[k])
+
+    def grad_store(p):
+        at = pl.ds(p * feats, feats)
+        return pltpu.make_async_copy(grad.at[:, at], grad_hbm.at[:, at], grad_out.at[p])
+
+    for p in range(PIECES):
+        for h in range(HALVES):
+            ret_load(p, h).start()
+    for k in range(parts):
+        w_load(k).start()
+    slots = lax.broadcasted_iota(jnp.int32, (NGROUP * CAP, tok), 0)
+    back = jnp.where(slots == dest_ref[0:1, :], 1.0, 0.0).T.astype(BF16)
+    for p in range(PIECES):
+        for h in range(HALVES):
+            ret_load(p, h).wait()
+        pieces = jnp.concatenate(
+            [ret[g // HALVES, (g % HALVES) * PIECES + p] for g in range(NGROUP)], 0
+        )
+        grad[:, p * feats:(p + 1) * feats] = jnp.dot(
+            back, pieces, preferred_element_type=F32
+        ).astype(BF16)
+        grad_store(p).start()
+        w_load(p).wait()
+        w_store(p).start()
+    for p in range(PIECES):
+        grad_store(p).wait()
+        w_store(p).wait()
+
+
+def finish(ret, dest, wgrad):
+    tok, feats = dest.shape[1], ret.shape[3]
+    dma = pltpu.SemaphoreType.DMA((PIECES,))
+    vmem = pl.BlockSpec(memory_space=pltpu.VMEM)
     hbm = pl.BlockSpec(memory_space=pl.ANY)
     return pl.pallas_call(
-        body,
-        out_shape=tuple(jax.ShapeDtypeStruct(v.shape, v.dtype) for v in values),
-        in_specs=[hbm] * len(values),
-        out_specs=(hbm,) * len(values),
-        scratch_shapes=[pltpu.SemaphoreType.DMA((len(values), parts))],
-        name="hand_over",
-    )(*values)
+        finish_kernel,
+        out_shape=(
+            jax.ShapeDtypeStruct((tok, PIECES * feats), BF16),
+            jax.ShapeDtypeStruct(wgrad.shape, BF16),
+        ),
+        in_specs=[vmem, hbm, hbm],
+        out_specs=(hbm, hbm),
+        scratch_shapes=[
+            pltpu.VMEM(ret.shape, BF16),
+            pltpu.VMEM((tok, PIECES * feats), BF16),
+            pltpu.VMEM(wgrad.shape, BF16),
+            pltpu.SemaphoreType.DMA((NZ,)), dma, dma, dma,
+        ],
+        name="finish",
+    )(dest, ret, wgrad)
 
 
 def per_device(attn_out, out_cot, modality, group_modality, o_weight):
-    return hand_over(
-        backward(modality.reshape(1, -1), group_modality, attn_out, out_cot, o_weight)
+    ret, dest, wgrad = backward(
+        modality.reshape(1, -1), group_modality, attn_out, out_cot, o_weight
     )
+    return finish(ret, dest, wgrad)
 
 
 def solution(mesh):

time: 233 us -> 172 us (0.74)
  Pallas kernels: 231 us -> 169 us
    pallas_call x2, Pallas kernels: 231 us -> 169 us  [the longest x1 165 us: backward(): pl.pallas_call(kernel, out_shape=(jax.ShapeDtypeStruct((NX, NZ, CAP, feat...]
where the time goes in v7:
time: 172 us; the launch traced here: 169 us
  Pallas kernels  169 us (98%)
    pallas_call x1, Pallas kernels, backward(): pl.pallas_call(kernel, out_shape=(jax.ShapeDtypeStruct((NX, NZ, CAP, feat...  165 us
    pallas_call x1, Pallas kernels, finish(): pl.pallas_call(finish_kernel, out_shape=(jax.ShapeDtypeStruct((tok, PIECE...  3.69 us

profile of v7, /device:TPU:8, one launch (start us, length us, event | category | flops | bytes accessed | tf_op | source)
XLA Modules:
  0.0 169.4 jit_solution(15988359349935689918)
XLA Ops:
  0.6 165.0 %moe_proj_backward.1 = (bf16[4,8,24,1024]{3,2,1,0:T(8,128)(2,1)}, s32[8,128]{1,0:T(8,128)}, bf16[1024,512]{1,0:T(8,128)(2,1)}) custom-call(s32[1,128]{1,0:T(1,128)} %bitcast.1, s32[8]{0:T(128)} %gm_ref.1, bf16[128,4096]{1,0:T(8,128)(2,1)} %attn_hbm.1, bf16[128,4096]{1,0:T(8,128)(2,1)} %cot_hbm.1, bf16[1024,4096]{1,0:T(8,128)(2,1)} %w_ref.1), custom_call_target="tpu_custom_call" | custom-call | tf_op jit(solution)/shard_map/moe_proj_backward/pallas_call | solution.py:439
  165.7 3.7 %finish.1 = (bf16[128,4096]{1,0:T(8,128)(2,1)}, bf16[1024,512]{1,0:T(8,128)(2,1)}) custom-call(s32[8,128]{1,0:T(8,128)} %get-tuple-element.5.dest_ref, bf16[4,8,24,1024]{3,2,1,0:T(8,128)(2,1)} %get-tuple-element.6.ret_hbm, bf16[1024,512]{1,0:T(8,128)(2,1)} %get-tuple-element.7.w_hbm), custom_call_target="tpu_custom_call" | custom-call | tf_op jit(solution)/shard_map/finish/pallas_call | solution.py:536

commit v8 on v7

--- a/solution.py
+++ b/solution.py
@@ -14,10 +14,12 @@
 NDP = 8
 CORES = 2
 NY = NDP // CORES
-SOURCES = ((0, -1, 1), (-2, 2), (-3, 3), (4,))
+ORDER = (0, -1, 1, -2, 2, -3, 3, 4)
+PARTS = ((0, 3), (3, 2), (5, 2), (7, 1))
 NC = 4
 LAST = NZ // 2
 TILE = 256
+PLACE = {off % NZ: at for at, off in enumerate(ORDER)}
 MESH = pl.DeviceIdType.MESH
 F32 = jnp.float32
 BF16 = jnp.bfloat16
@@ -169,19 +171,19 @@
 
     def attn_z_copy(k):
         return remote(
-            attn_z_src(k), attn_got.at[:, my_z], az_send.at[k], az_recv.at[NZ - k], at_z(k)
+            attn_z_src(k), attn_got.at[:, PLACE[NZ - k]], az_send.at[k], az_recv.at[NZ - k], at_z(k)
         )
 
     def attn_along_z():
         own_ax.wait()
         for k in range(1, NX):
             attn_x_copy(k).wait_recv()
-        pltpu.make_async_copy(attn_z_src(0), attn_got.at[:, my_z], az_own).start()
+        pltpu.make_async_copy(attn_z_src(0), attn_got.at[:, 0], az_own).start()
         for k in range(1, NZ):
             attn_z_copy(k).start()
 
     def attn_arrived():
-        pltpu.make_async_copy(attn_z_src(0), attn_got.at[:, my_z], az_own).wait()
+        pltpu.make_async_copy(attn_z_src(0), attn_got.at[:, 0], az_own).wait()
         for k in range(1, NZ):
             attn_z_copy(k).wait_recv()
 
@@ -194,26 +196,24 @@
     x_of = sum((rows >= CAP * k).astype(jnp.int32) for k in range(1, NX))
     wanted = rows + CAP * (HALVES - 1) * x_of + CAP * my_half
 
-    def deliver(c, off):
-        slot = off % NZ
-        pick = jnp.where(wanted == dests[slot, 0:1, :], 1.0, 0.0).astype(BF16)
-        got = jnp.dot(pick, ring[c, slot], preferred_element_type=F32).astype(BF16)
-        for x in range(NX):
-            staged[c, x, slot] = got[x * CAP:(x + 1) * CAP]
-        part = abs(off) - 1 if off else 0
-        lands = cot_got.at[c, my_x, (my_z + off + NZ) % NZ]
-        for k in range(NX):
-            src = staged.at[c, (my_x + k) % NX, slot]
-            if k == 0:
-                pltpu.make_async_copy(src, lands, x_own.at[c, part]).start()
-            else:
-                remote(
-                    src, lands, x_send.at[c, k], x_recv.at[c, part, NX - k], at_x(k)
-                ).start()
+    def deliver(c, *offsets):
+        at = pl.ds(PLACE[offsets[0] % NZ], len(offsets))
+        for off in offsets:
+            slot = off % NZ
+            pick = jnp.where(wanted == dests[slot, 0:1, :], 1.0, 0.0).astype(BF16)
+            got = jnp.dot(pick, ring[c, slot], preferred_element_type=F32).astype(BF16)
+            for x in range(NX):
+                staged[c, x, PLACE[slot]] = got[x * CAP:(x + 1) * CAP]
+        part = max(abs(offsets[0]), 1) - 1
+        lands = cot_got.at[c, my_x, at]
+        for k in range(1, NX):
+            src = staged.at[c, (my_x + k) % NX, at]
+            remote(src, lands, x_send.at[c, k], x_recv.at[c, part, NX - k], at_x(k)).start()
+        pltpu.make_async_copy(staged.at[c, my_x, at], lands, x_own.at[c, part]).start()
 
     def arrived(c, parts):
         for part in parts:
-            count = len(SOURCES[part])
+            count = PARTS[part][1]
             wait_bytes(staged.at[c, 0, pl.ds(0, count)], x_own.at[c, part])
             for k in range(1, NX):
                 wait_bytes(staged.at[c, k, pl.ds(0, count)], x_recv.at[c, part, k])
@@ -238,27 +238,26 @@
         for d in range(NDP):
             w_load(c + 2, d).start()
 
-    def rows_grad(offsets):
-        zs = [(my_z + off + NZ) % NZ for off in offsets]
-        count = NX * CAP
+    def rows_grad(part):
+        first, count = PARTS[part]
+        own = slice(first, first + count)
 
         @pl.loop(0, feats // TILE)
         def _(j):
             at = pl.ds(pl.multiple_of(j * TILE, TILE), TILE)
             term = sum(
                 lax.dot_general(
-                    jnp.concatenate([cot_got[c, :, z].reshape(count, width) for z in zs], 0),
-                    w_chunk[c % 2, at, :], (((1,), (1,)), ((), ())), preferred_element_type=F32,
+                    cot_got[c, :, own].reshape(NX * count * CAP, width), w_chunk[c % 2, at, :],
+                    (((1,), (1,)), ((), ())), preferred_element_type=F32,
                 )
                 for c in range(NC - 2, NC)
             )
-            for i, z in enumerate(zs):
-                total = term[i * count:(i + 1) * count].reshape(NX, CAP, TILE) + acc[:, z, :, at]
-                grads[:, z, :, at] = total.astype(BF16)
-
-        for off in offsets:
+            total = term.reshape(NX, count, CAP, TILE) + acc[:, own, :, at]
+            grads[:, own, :, at] = total.astype(BF16)
+
+        for off in ORDER[own]:
             if off == 0:
-                pltpu.make_async_copy(grads.at[:, my_z], ret_z.at[my_z], rz_own).start()
+                pltpu.make_async_copy(grads.at[:, 0], ret_z.at[my_z], rz_own).start()
             else:
                 ret_z_copy(off % NZ).start()
 
@@ -330,31 +329,29 @@
 
     def ret_z_copy(k):
         return remote(
-            grads.at[:, (my_z + k) % NZ], ret_z.at[my_z], rz_send.at[k], rz_recv.at[NZ - k], at_z(k)
+            grads.at[:, PLACE[k]], ret_z.at[my_z], rz_send.at[k], rz_recv.at[NZ - k], at_z(k)
         )
 
     def ring_step(c, s):
         if c >= 2 and s == 0:
             wait_bytes(ring.at[c, 0], cot_in.at[c])
-        if s > 0:
-            ring_copy(c, s - 1, True).wait_recv()
-            ring_copy(c, s - 1, False).wait_recv()
-        if s < LAST and (c >= 2 or s > 0):
-            ring_copy(c, s, True).start()
-            ring_copy(c, s, False).start()
+        for right in (True, False):
+            if s > 0:
+                ring_copy(c, s - 1, right).wait_recv()
+            if s < LAST and (c >= 2 or s > 0):
+                ring_copy(c, s, right).start()
         if (c, s) == (0, 1):
             for k in range(1, NZ):
                 dest_copy(k).wait_recv()
         if s in (0, LAST):
             deliver(c, s)
         else:
-            deliver(c, -s)
-            deliver(c, s)
+            deliver(c, -s, s)
 
     for c, s in ((0, 0), (1, 0), (0, 1), (1, 1), (0, 2)):
         ring_step(c, s)
     attn_along_z()
-    every = range(len(SOURCES))
+    every = range(len(PARTS))
     for c, s in ((1, 2), (0, 3), (2, 0), (1, 3), (3, 0), (0, 4), (2, 1), (1, 4)):
         ring_step(c, s)
     arrived(0, every)
@@ -372,21 +369,21 @@
     for c in range(NC - 2, NC):
         wait_bytes(w_chunk.at[c % 2], w_sem.at[c])
         arrived(c, (0,))
-    rows_grad(SOURCES[0])
+    rows_grad(0)
     ring_step(3, 3)
     weight_pair(1)
     for c in range(NC - 2, NC):
         arrived(c, (1,))
-    rows_grad(SOURCES[1])
+    rows_grad(1)
     ring_step(2, 4)
     for c in range(NC - 2, NC):
         arrived(c, (2,))
-    rows_grad(SOURCES[2])
+    rows_grad(2)
     ring_step(3, 4)
     arrived(2, (3,))
     weight_grad(2)
     arrived(3, (3,))
-    rows_grad(SOURCES[3])
+    rows_grad(3)
     weight_pair(2)
     weight_grad(3)
     weight_pair(3)
@@ -401,7 +398,7 @@
             else:
                 remote(src, dst, rx_send.at[k], rx_recv.at[NX - k], at_x(k)).start()
 
-    pltpu.make_async_copy(grads.at[:, my_z], ret_z.at[my_z], rz_own).wait()
+    pltpu.make_async_copy(grads.at[:, 0], ret_z.at[my_z], rz_own).wait()
     ret_x_start(my_z)
     for k in (1, 7, 2, 6, 3, 5, 4):
         ret_z_copy(k).wait_recv()

time: 172 us -> 172 us (level)
  no operation moved by 1% of the time
where the time goes in v8:
time: 172 us; the launch traced here: 169 us
  Pallas kernels  169 us (98%)
    pallas_call x1, Pallas kernels, backward(): pl.pallas_call(kernel, out_shape=(jax.ShapeDtypeStruct((NX, NZ, CAP, feat...  165 us
    pallas_call x1, Pallas kernels, finish(): pl.pallas_call(finish_kernel, out_shape=(jax.ShapeDtypeStruct((tok, PIECE...  3.69 us

profile of v8, /device:TPU:8, one launch (start us, length us, event | category | flops | bytes accessed | tf_op | source)
XLA Modules:
  0.0 169.4 jit_solution(13740535242083842259)
XLA Ops:
  0.6 165.0 %moe_proj_backward.1 = (bf16[4,8,24,1024]{3,2,1,0:T(8,128)(2,1)}, s32[8,128]{1,0:T(8,128)}, bf16[1024,512]{1,0:T(8,128)(2,1)}) custom-call(s32[1,128]{1,0:T(1,128)} %bitcast.1, s32[8]{0:T(128)} %gm_ref.1, bf16[128,4096]{1,0:T(8,128)(2,1)} %attn_hbm.1, bf16[128,4096]{1,0:T(8,128)(2,1)} %cot_hbm.1, bf16[1024,4096]{1,0:T(8,128)(2,1)} %w_ref.1), custom_call_target="tpu_custom_call" | custom-call | tf_op jit(solution)/shard_map/moe_proj_backward/pallas_call | solution.py:436
  165.7 3.7 %finish.1 = (bf16[128,4096]{1,0:T(8,128)(2,1)}, bf16[1024,512]{1,0:T(8,128)(2,1)}) custom-call(s32[8,128]{1,0:T(8,128)} %get-tuple-element.5.dest_ref, bf16[4,8,24,1024]{3,2,1,0:T(8,128)(2,1)} %get-tuple-element.6.ret_hbm, bf16[1024,512]{1,0:T(8,128)(2,1)} %get-tuple-element.7.w_hbm), custom_call_target="tpu_custom_call" | custom-call | tf_op jit(solution)/shard_map/finish/pallas_call | solution.py:533

commit v9 on v8

--- a/solution.py
+++ b/solution.py
@@ -436,14 +436,14 @@
     return pl.pallas_call(
         kernel,
         out_shape=(
-            jax.ShapeDtypeStruct((NX, NZ, CAP, feats), BF16),
-            jax.ShapeDtypeStruct((8, tok), jnp.int32),
-            jax.ShapeDtypeStruct((feats, model // NDP), BF16),
+            pltpu.VMEM((NX, NZ, CAP, feats), BF16),
+            pltpu.VMEM((8, tok), jnp.int32),
+            pltpu.VMEM((feats, model // NDP), BF16),
         ),
         in_specs=[
             vmem, pl.BlockSpec(memory_space=pltpu.SMEM), hbm, hbm, hbm,
         ],
-        out_specs=(hbm, vmem, vmem),
+        out_specs=(vmem, vmem, vmem),
         scratch_shapes=[
             pltpu.VMEM((tok, model), BF16),
             pltpu.VMEM((NC, NZ, tok, width), BF16),
@@ -472,45 +472,24 @@
             dma((NX,)), dma((NX,)), dma,
         ],
         compiler_params=pltpu.CompilerParams(
-            collective_id=0, has_side_effects=True, vmem_limit_bytes=63 * 1024 * 1024
+            collective_id=0, has_side_effects=True, vmem_limit_bytes=58 * 1024 * 1024
         ),
         name="moe_proj_backward",
     )(mod, gm, attn, cot, w)
 
 
-def finish_kernel(
-    dest_ref, ret_hbm, w_hbm, grad_hbm, w_out, ret, grad, wgrad, ret_in, grad_out, w_in, w_sent,
-):
+def finish_kernel(dest_ref, ret, wgrad, grad_hbm, w_out, grad, grad_out, w_sent):
     tok, feats = dest_ref.shape[1], ret.shape[3]
-    parts = w_in.shape[0]
-    rows = wgrad.shape[0] // parts
-
-    def ret_load(p, h):
-        at = h * PIECES + p
-        return pltpu.make_async_copy(ret_hbm.at[:, at], ret.at[:, at], ret_in.at[at])
-
-    def w_load(k):
-        at = pl.ds(k * rows, rows)
-        return pltpu.make_async_copy(w_hbm.at[at], wgrad.at[at], w_in.at[k])
-
-    def w_store(k):
-        at = pl.ds(k * rows, rows)
-        return pltpu.make_async_copy(wgrad.at[at], w_out.at[at], w_sent.at[k])
+    w_store = pltpu.make_async_copy(wgrad, w_out, w_sent)
+    w_store.start()
 
     def grad_store(p):
         at = pl.ds(p * feats, feats)
         return pltpu.make_async_copy(grad.at[:, at], grad_hbm.at[:, at], grad_out.at[p])
 
-    for p in range(PIECES):
-        for h in range(HALVES):
-            ret_load(p, h).start()
-    for k in range(parts):
-        w_load(k).start()
     slots = lax.broadcasted_iota(jnp.int32, (NGROUP * CAP, tok), 0)
     back = jnp.where(slots == dest_ref[0:1, :], 1.0, 0.0).T.astype(BF16)
     for p in range(PIECES):
-        for h in range(HALVES):
-            ret_load(p, h).wait()
         pieces = jnp.concatenate(
             [ret[g // HALVES, (g % HALVES) * PIECES + p] for g in range(NGROUP)], 0
         )
@@ -518,16 +497,13 @@
             back, pieces, preferred_element_type=F32
         ).astype(BF16)
         grad_store(p).start()
-        w_load(p).wait()
-        w_store(p).start()
+    w_store.wait()
     for p in range(PIECES):
         grad_store(p).wait()
-        w_store(p).wait()
 
 
 def finish(ret, dest, wgrad):
     tok, feats = dest.shape[1], ret.shape[3]
-    dma = pltpu.SemaphoreType.DMA((PIECES,))
     vmem = pl.BlockSpec(memory_space=pltpu.VMEM)
     hbm = pl.BlockSpec(memory_space=pl.ANY)
     return pl.pallas_call(
@@ -536,14 +512,13 @@
             jax.ShapeDtypeStruct((tok, PIECES * feats), BF16),
             jax.ShapeDtypeStruct(wgrad.shape, BF16),
         ),
-        in_specs=[vmem, hbm, hbm],
+        in_specs=[vmem, vmem, vmem],
         out_specs=(hbm, hbm),
         scratch_shapes=[
-            pltpu.VMEM(ret.shape, BF16),
             pltpu.VMEM((tok, PIECES * feats), BF16),
-            pltpu.VMEM(wgrad.shape, BF16),
-            pltpu.SemaphoreType.DMA((NZ,)), dma, dma, dma,
+            pltpu.SemaphoreType.DMA((PIECES,)), pltpu.SemaphoreType.DMA,
         ],
+        compiler_params=pltpu.CompilerParams(vmem_limit_bytes=16 * 1024 * 1024),
         name="finish",
     )(dest, ret, wgrad)
 

time: 172 us -> 168 us (0.977)
  Pallas kernels: 169 us -> 165 us
    pallas_call x1, Pallas kernels: 3.69 us -> 1.35 us  [finish(): pl.pallas_call(finish_kernel, out_shape=(jax.ShapeDtypeStruct((tok, PIECE...]
where the time goes in v9:
time: 168 us; the launch traced here: 166 us
  Pallas kernels  165 us (98%)
    pallas_call x1, Pallas kernels, backward(): pl.pallas_call(kernel, out_shape=(pltpu.VMEM((NX, NZ, CAP, feats), BF16),...  164 us

profile of v9, /device:TPU:8, one launch (start us, length us, event | category | flops | bytes accessed | tf_op | source)
XLA Modules:
  0.0 166.0 jit_solution(1713885879378520422)
XLA Ops:
  0.6 164.0 %moe_proj_backward.1 = (bf16[4,8,24,1024]{3,2,1,0:T(8,128)(2,1)S(1)}, s32[8,128]{1,0:T(8,128)S(1)}, bf16[1024,512]{1,0:T(8,128)(2,1)S(1)}) custom-call(s32[1,128]{1,0:T(1,128)} %bitcast.1, s32[8]{0:T(128)} %gm_ref.1, bf16[128,4096]{1,0:T(8,128)(2,1)} %attn_hbm.1, bf16[128,4096]{1,0:T(8,128)(2,1)} %cot_hbm.1, bf16[1024,4096]{1,0:T(8,128)(2,1)} %w_ref.1), custom_call_target="tpu_custom_call" | custom-call | tf_op jit(solution)/shard_map/moe_proj_backward/pallas_call | solution.py:436
  164.7 1.4 finish.1

commit v10 on v9

--- a/solution.py
+++ b/solution.py
@@ -302,16 +302,19 @@
     def weight_pair(c):
         pair_copy(c).wait_recv()
 
-        @pl.loop(0, feats // TILE)
-        def _(j):
-            at = pl.ds(pl.multiple_of(j * TILE, TILE), TILE)
-            for y in range(NY):
+        for k in (1, 2, 3, 0):
+            y = (my_y + k) % NY
+
+            @pl.loop(0, feats // TILE)
+            def _(j):
+                at = pl.ds(pl.multiple_of(j * TILE, TILE), TILE)
                 both = partial[c % 2, my_core, y, at, :].astype(F32) + other[c, y, at, :].astype(F32)
                 partial[c % 2, my_core, y, at, :] = both.astype(BF16)
 
-        rs_own_copy(c).start()
-        for k in range(1, NY):
-            rs_copy(c, k).start()
+            if k == 0:
+                rs_own_copy(c).start()
+            else:
+                rs_copy(c, k).start()
 
     def weight_grad_sum(c):
         if c >= NC - 2:
@@ -372,20 +375,19 @@
     rows_grad(0)
     ring_step(3, 3)
     weight_pair(1)
+    ring_step(2, 4)
     for c in range(NC - 2, NC):
         arrived(c, (1,))
     rows_grad(1)
-    ring_step(2, 4)
-    for c in range(NC - 2, NC):
-        arrived(c, (2,))
+    arrived(2, (2, 3))
+    weight_grad(2)
+    arrived(3, (2,))
     rows_grad(2)
     ring_step(3, 4)
-    arrived(2, (3,))
-    weight_grad(2)
+    weight_pair(2)
     arrived(3, (3,))
+    weight_grad(3)
     rows_grad(3)
-    weight_pair(2)
-    weight_grad(3)
     weight_pair(3)
     weight_grad_sum(0)
     weight_grad_sum(1)

time: 168 us -> 168 us (level)
  no operation moved by 1% of the time
where the time goes in v10:
time: 168 us; the launch traced here: 166 us
  Pallas kernels  165 us (98%)
    pallas_call x1, Pallas kernels, backward(): pl.pallas_call(kernel, out_shape=(pltpu.VMEM((NX, NZ, CAP, feats), BF16),...  164 us

profile of v10, /device:TPU:8, one launch (start us, length us, event | category | flops | bytes accessed | tf_op | source)
XLA Modules:
  0.0 165.9 jit_solution(149129712225539858)
XLA Ops:
  0.6 163.9 %moe_proj_backward.1 = (bf16[4,8,24,1024]{3,2,1,0:T(8,128)(2,1)S(1)}, s32[8,128]{1,0:T(8,128)S(1)}, bf16[1024,512]{1,0:T(8,128)(2,1)S(1)}) custom-call(s32[1,128]{1,0:T(1,128)} %bitcast.1, s32[8]{0:T(128)} %gm_ref.1, bf16[128,4096]{1,0:T(8,128)(2,1)} %attn_hbm.1, bf16[128,4096]{1,0:T(8,128)(2,1)} %cot_hbm.1, bf16[1024,4096]{1,0:T(8,128)(2,1)} %w_ref.1), custom_call_target="tpu_custom_call" | custom-call | tf_op jit(solution)/shard_map/moe_proj_backward/pallas_call | solution.py:438
  164.6 1.4 finish.1

commit v11 on v10

--- a/solution.py
+++ b/solution.py
@@ -89,8 +89,8 @@
         pl.semaphore_signal(barrier, inc=1, device_id=at_y(k), device_id_type=MESH)
     pl.semaphore_signal(barrier, inc=1, device_id=other_core, device_id_type=MESH)
 
-    own_block(0)
-    own_block(1)
+    for c in range(3):
+        own_block(c)
     attn_load.start()
     pl.semaphore_wait(barrier, NZ - 1 + NX - 1 + NY)
 
@@ -108,12 +108,14 @@
             at_z(1 if right else -1),
         )
 
-    for c in range(2):
+    def ring_start(c):
         wait_bytes(ring.at[c, 0], cot_in.at[c])
         ring_copy(c, 0, True).start()
         ring_copy(c, 0, False).start()
-    for c in range(2, NC):
-        own_block(c)
+
+    for c in range(3):
+        ring_start(c)
+    own_block(3)
     for c in range(2):
         for d in range(NDP):
             w_load(c, d).start()
@@ -336,12 +338,10 @@
         )
 
     def ring_step(c, s):
-        if c >= 2 and s == 0:
-            wait_bytes(ring.at[c, 0], cot_in.at[c])
         for right in (True, False):
             if s > 0:
                 ring_copy(c, s - 1, right).wait_recv()
-            if s < LAST and (c >= 2 or s > 0):
+            if 0 < s < LAST:
                 ring_copy(c, s, right).start()
         if (c, s) == (0, 1):
             for k in range(1, NZ):
@@ -351,8 +351,10 @@
         else:
             deliver(c, -s, s)
 
-    for c, s in ((0, 0), (1, 0), (0, 1), (1, 1), (0, 2)):
+    for c, s in ((0, 0), (1, 0), (0, 1), (1, 1)):
         ring_step(c, s)
+    ring_start(3)
+    ring_step(0, 2)
     attn_along_z()
     every = range(len(PARTS))
     for c, s in ((1, 2), (0, 3), (2, 0), (1, 3), (3, 0), (0, 4), (2, 1), (1, 4)):

time: 168 us -> 173 us (1.030); the launches traced: 166 us -> 173 us
  Pallas kernels: 165 us -> 172 us
    pallas_call x1, Pallas kernels: 164 us -> 171 us  [backward(): pl.pallas_call(kernel, out_shape=(pltpu.VMEM((NX, NZ, CAP, feats), BF16),...]
where the time goes in v11:
time: 173 us
  Pallas kernels  172 us (99%)
    pallas_call x1, Pallas kernels, backward(): pl.pallas_call(kernel, out_shape=(pltpu.VMEM((NX, NZ, CAP, feats), BF16),...  171 us

profile of v11, /device:TPU:8, one launch (start us, length us, event | category | flops | bytes accessed | tf_op | source)
XLA Modules:
  0.0 172.9 jit_solution(5681342200679986024)
XLA Ops:
  0.6 171.0 %moe_proj_backward.1 = (bf16[4,8,24,1024]{3,2,1,0:T(8,128)(2,1)S(1)}, s32[8,128]{1,0:T(8,128)S(1)}, bf16[1024,512]{1,0:T(8,128)(2,1)S(1)}) custom-call(s32[1,128]{1,0:T(1,128)} %bitcast.1, s32[8]{0:T(128)} %gm_ref.1, bf16[128,4096]{1,0:T(8,128)(2,1)} %attn_hbm.1, bf16[128,4096]{1,0:T(8,128)(2,1)} %cot_hbm.1, bf16[1024,4096]{1,0:T(8,128)(2,1)} %w_ref.1), custom_call_target="tpu_custom_call" | custom-call | tf_op jit(solution)/shard_map/moe_proj_backward/pallas_call | solution.py:440
  171.6 1.4 finish.1

commit v12 on v10

--- a/solution.py
+++ b/solution.py
@@ -179,7 +179,7 @@
         for k in range(1, NX):
             attn_x_copy(k).wait_recv()
         pltpu.make_async_copy(attn_z_src(0), attn_got.at[:, 0], az_own).start()
-        for k in range(1, NZ):
+        for k in (3, 4, 5):
             attn_z_copy(k).start()
 
     def attn_arrived():
@@ -355,7 +355,11 @@
         ring_step(c, s)
     attn_along_z()
     every = range(len(PARTS))
-    for c, s in ((1, 2), (0, 3), (2, 0), (1, 3), (3, 0), (0, 4), (2, 1), (1, 4)):
+    for c, s in ((1, 2), (0, 3), (2, 0), (1, 3), (3, 0)):
+        ring_step(c, s)
+    for k in (1, 2, 6, 7):
+        attn_z_copy(k).start()
+    for c, s in ((0, 4), (2, 1), (1, 4)):
         ring_step(c, s)
     arrived(0, every)
     input_grad(0)

time: 168 us -> 168 us (level)
  no operation moved by 1% of the time
where the time goes in v12:
time: 168 us; the launch traced here: 166 us
  Pallas kernels  165 us (98%)
    pallas_call x1, Pallas kernels, backward(): pl.pallas_call(kernel, out_shape=(pltpu.VMEM((NX, NZ, CAP, feats), BF16),...  164 us

profile of v12, /device:TPU:8, one launch (start us, length us, event | category | flops | bytes accessed | tf_op | source)
XLA Modules:
  0.0 165.9 jit_solution(934740742087390707)
XLA Ops:
  0.6 163.9 %moe_proj_backward.1 = (bf16[4,8,24,1024]{3,2,1,0:T(8,128)(2,1)S(1)}, s32[8,128]{1,0:T(8,128)S(1)}, bf16[1024,512]{1,0:T(8,128)(2,1)S(1)}) custom-call(s32[1,128]{1,0:T(1,128)} %bitcast.1, s32[8]{0:T(128)} %gm_ref.1, bf16[128,4096]{1,0:T(8,128)(2,1)} %attn_hbm.1, bf16[128,4096]{1,0:T(8,128)(2,1)} %cot_hbm.1, bf16[1024,4096]{1,0:T(8,128)(2,1)} %w_ref.1), custom_call_target="tpu_custom_call" | custom-call | tf_op jit(solution)/shard_map/moe_proj_backward/pallas_call | solution.py:442
  164.6 1.4 finish.1
